TPU v7x, 128 devices: a whole 4x4x4 slice. The times are simulated.
128 devices in a mesh: seq: 32 (over y, z, core), head: 4 (over x).
Axes of the slice: x: 4, y: 4, z: 4, core: 2. Of those that a mesh axis runs over, the one named last changes fastest.
Arguments:
- vision: bfloat16 [65536, 7680], P(('seq', 'head')), may hold values from -6 to 6
- w_key: bfloat16 [7680, 512], replicated, may hold values from -0.0625 to 0.0625
- w_value: bfloat16 [7680, 512], replicated, may hold values from -0.0625 to 0.0625
- queries: bfloat16 [256, 4096], P('seq', 'head'), may hold values from -240 to 240
- w_out: bfloat16 [4096, 8192], P('head', 'seq'), may hold values from -0.09375 to 0.09375
Outputs:
- mixed: bfloat16 [256, 8192], P('head', 'seq')
All inputs are finite; a program needn't handle non-finite values.
Results may differ from a plain program's by a relative error of at most 0.03.
Values may be sent and summed in bfloat16 or wider, within the bound.
No kernel may reach another device: no remote copies, remote signals or barrier semaphores. Data moves between devices by JAX's collectives and lax.ppermute only.
A program may use at most 128 MiB of HBM per device.

v0:
```python
import jax
import jax.numpy as jnp
from jax import lax
from jax.sharding import PartitionSpec as P

HD = 128


def scale_rows(partial_value, factor):
    return (
        partial_value.reshape(factor.shape[0], factor.shape[1], -1) * factor[:, :, None]
    ).reshape(factor.shape[0], -1)


def divide_rows(partial_value, denom):
    return (partial_value.reshape(denom.shape[0], denom.shape[1], -1) / denom[:, :, None]).reshape(
        denom.shape[0], -1
    )


def attend(queries_all, keys_here, values_here):
    head_size = HD
    kv_local = keys_here.shape[1] // head_size
    text_rows = queries_all.shape[0]
    q_heads = queries_all.shape[1] // head_size
    group_size = q_heads // kv_local
    grouped = queries_all.reshape(text_rows, kv_local, group_size, head_size)
    key_heads = keys_here.reshape(keys_here.shape[0], kv_local, head_size)
    value_heads = values_here.reshape(values_here.shape[0], kv_local, head_size)
    scores = jnp.einsum(
        "tkgd,nkd->kgtn", grouped, key_heads, preferred_element_type=jnp.float32
    ) * head_size ** (-0.5)
    maxima = jnp.max(scores, axis=-1)
    powers = jnp.exp(scores - maxima[..., None])
    totals = jnp.sum(powers, axis=-1)
    partial_value = jnp.einsum(
        "kgtn,nkd->tkgd",
        powers.astype(jnp.bfloat16),
        value_heads,
        preferred_element_type=jnp.float32,
    )
    partial_value = partial_value.reshape(text_rows, q_heads * head_size)
    maxima = maxima.transpose(2, 0, 1).reshape(text_rows, q_heads)
    totals = totals.transpose(2, 0, 1).reshape(text_rows, q_heads)
    return (maxima, totals, partial_value)


def shards(vision, w_key, w_value, queries, w_out):
    keys = jnp.dot(vision, w_key, preferred_element_type=jnp.float32).astype(jnp.bfloat16)
    values = jnp.dot(vision, w_value, preferred_element_type=jnp.float32).astype(jnp.bfloat16)
    keys_here, values_here = (
        lax.all_to_all(keys, "head", split_axis=1, concat_axis=0, tiled=True),
        lax.all_to_all(values, "head", split_axis=1, concat_axis=0, tiled=True),
    )
    queries_all = lax.all_gather(queries, "seq", axis=0, tiled=True)
    maxima, totals, partial_value = attend(queries_all, keys_here, values_here)
    global_max = lax.pmax(maxima, "seq")
    factor = jnp.exp(maxima - global_max)
    denom, numer = (
        lax.psum((totals * factor).astype(jnp.bfloat16), "seq").astype(jnp.float32),
        lax.psum(scale_rows(partial_value, factor).astype(jnp.bfloat16), "seq").astype(jnp.float32),
    )
    attended = divide_rows(numer, denom).astype(jnp.bfloat16)
    return lax.psum_scatter(
        jnp.dot(attended, w_out, preferred_element_type=jnp.float32).astype(jnp.bfloat16),
        "head",
        scatter_dimension=0,
        tiled=True,
    )


def solution(mesh):
    placed = (P(("seq", "head"), None), P(), P(), P("seq", "head"), P("head", "seq"))
    return jax.shard_map(
        shards, mesh=mesh, in_specs=placed, out_specs=P("head", "seq"), check_vma=False
    )
```

profile of v0, /device:TPU:0, one launch (start us, length us, event | category | flops | bytes accessed | tf_op | source)
XLA Modules:
  0.0 286.8 jit_solution(6718358822578115209)
XLA Ops:
  6.5 0.0 copy-start
  6.5 10.6 %convolution_convert_fusion.1 = bf16[512,512]{0,1:T(8,128)(2,1)} fusion(bf16[512,7680]{1,0:T(8,128)(2,1)} %param.5, bf16[7680,512]{1,0:T(8,128)(2,1)} %param.7), kind=kOutput, calls=%fused_computation.8 | convolution fusion | flops 4026793984 | bytes 16252928 | tf_op jit(solution)/shard_map/dot_general | solution.py:50
  17.1 0.0 copy-start.1
  17.1 4.5 %all-to-all-start = ((bf16[512,4,128]{0,2,1:T(8,128)(2,1)}), bf16[512,4,128]{0,2,1:T(8,128)(2,1)S(1)}, u32[]{:S(2)}, u32[]{:S(2)}) async-start(bf16[512,4,128]{0,2,1:T(8,128)(2,1)} %bitcast), calls=%async_computation | async-start | bytes 1048576 | tf_op jit(solution)/shard_map/all_to_all | solution.py:53
  21.7 10.5 %convolution_convert_fusion = bf16[512,512]{0,1:T(8,128)(2,1)} fusion(bf16[512,7680]{1,0:T(8,128)(2,1)} %param.5, bf16[7680,512]{1,0:T(8,128)(2,1)} %param.6), kind=kOutput, calls=%fused_computation.7 | convolution fusion | flops 4026793984 | bytes 16252928 | tf_op jit(solution)/shard_map/dot_general | solution.py:49
  32.2 0.0 all-to-all-done
  32.2 4.8 %all-to-all-start.1 = ((bf16[512,4,128]{0,2,1:T(8,128)(2,1)}), bf16[512,4,128]{0,2,1:T(8,128)(2,1)S(1)}, u32[]{:S(2)}, u32[]{:S(2)}) async-start(bf16[512,4,128]{0,2,1:T(8,128)(2,1)} %bitcast.2), calls=%async_computation.1 | async-start | bytes 1048576 | tf_op jit(solution)/shard_map/all_to_all | solution.py:52
  37.0 0.0 all-reduce.2.cloned.1.call-start
  37.0 0.0 copy-done.1
  37.0 26.5 %all_gather.3 = bf16[256,1024]{1,0:T(8,128)(2,1)S(1)} all-gather(bf16[8,1024]{1,0:T(8,128)(2,1)S(1)} %copy-done.1), channel_id=1, replica_groups=mesh['seq'=32,'head'=4] {'seq'}, dimensions={0}, use_global_device_ids=true | all-gather | bytes 540672 | tf_op jit(solution)/shard_map/all_gather | solution.py:55
  63.5 0.2 copy.16
  63.7 0.4 copy.14
  64.1 0.4 reshape.57
  64.5 0.0 all-to-all-done.1
  64.5 0.3 copy.15
  64.8 8.0 %bitcast_reduce_fusion = (f32[8,256]{1,0:T(8,128)S(1)}, f32[2048,256,8]{1,0,2:T(8,128)}) fusion(bf16[2048,128,1]{1,0,2:T(8,128)(2,1)S(1)} %bitcast.66, bf16[256,8,128]{0,2,1:T(8,128)(2,1)S(1)} %bitcast.65), kind=kOutput, calls=%fused_computation.1 | convolution fusion | flops 1082128384 | bytes 17833984 | tf_op jit(solution)/shard_map/tkgd,nkd->kgtn/dot_general | solution.py:30
  72.8 8.5 %fusion.1 = f32[8,256]{1,0:T(8,128)S(1)} fusion(f32[2048,256,8]{1,0,2:T(8,128)} %get-tuple-element.8, f32[8,256]{1,0:T(8,128)S(1)} %get-tuple-element.7), kind=kLoop, calls=%fused_computation.3 | loop fusion | flops 12580864 | bytes 16793600 | tf_op jit(solution)/shard_map/reduce_sum | solution.py:35
  81.3 7.4 %fusion.4 = f32[128,8,256]{2,0,1:T(8,128)S(1)} fusion(bf16[2048,128,1]{0,1,2:T(8,128)(2,1)S(1)} %reshape.57, f32[2048,256,8]{1,0,2:T(8,128)} %get-tuple-element.8, f32[8,256]{1,0:T(8,128)S(1)} %get-tuple-element.7), kind=kOutput, calls=%fused_computation.6 | convolution fusion | flops 1086324736 | bytes 18358272 | tf_op jit(solution)/shard_map/kgtn,nkd->tkgd/dot_general | solution.py:36
  88.7 66.3 %pmax.7 = f32[256,8]{0,1:T(8,128)S(1)} all-reduce(f32[256,8]{0,1:T(8,128)S(1)} %bitcast.69), channel_id=1, replica_groups=mesh['seq'=32,'head'=4] {'seq'}, use_global_device_ids=true, to_apply=%region_1.0 | all-reduce | flops 2048 | bytes 16384 | tf_op jit(solution)/shard_map/pmax | solution.py:57
  155.1 0.9 fusion.6
  156.0 0.0 all-reduce.2.cloned.1.call-update
  156.0 0.0 reduce-scatter.2.cloned.1.call-start
  156.0 62.8 %psum.15 = bf16[256,8]{0,1:T(8,128)(2,1)S(1)} all-reduce(bf16[256,8]{0,1:T(8,128)(2,1)S(1)} %get-tuple-element.5), channel_id=1, replica_groups=mesh['seq'=32,'head'=4] {'seq'}, use_global_device_ids=true, to_apply=%region_4.0 | all-reduce | flops 2048 | bytes 8192 | tf_op jit(solution)/shard_map/psum | solution.py:60
  218.8 38.6 %all-reduce.2.cloned.1.call-done = bf16[256,1024]{0,1:T(8,128)(2,1)} async-done(((bf16[256,1024]{0,1:T(8,128)(2,1)}), bf16[256,1024]{0,1:T(8,128)(2,1)}) %all-reduce.2.cloned.1.call-update) | async-done | bytes 524304 | tf_op jit(solution)/shard_map/psum | solution.py:61
  257.4 1.1 fusion.7
  258.6 0.0 copy-done
  258.6 1.0 convolution_convert_fusion.2
  259.6 0.0 reduce-scatter.2.cloned.1.call-update
  259.6 20.4 %reduce-scatter.2.cloned.1.call-done = bf16[64,256]{1,0:T(8,128)(2,1)} async-done(((bf16[256,256]{1,0:T(8,128)(2,1)}), bf16[64,256]{1,0:T(8,128)(2,1)}) %reduce-scatter.2.cloned.1.call-update) | async-done | bytes 32784 | tf_op jit(solution)/shard_map/reduce_scatter | solution.py:64
  (2 shorter events, 0.0 us)
Async XLA Ops:
  6.5 252.0 %copy-start = (bf16[1024,256]{1,0:T(8,128)(2,1)S(1)}, bf16[1024,256]{1,0:T(8,128)(2,1)}, u32[]{:S(2)}) copy-start(bf16[1024,256]{1,0:T(8,128)(2,1)} %param.9) | copy-start | bytes 1572868
  17.1 19.9 %copy-start.1 = (bf16[8,1024]{1,0:T(8,128)(2,1)S(1)}, bf16[8,1024]{1,0:T(8,128)(2,1)}, u32[]{:S(2)}) copy-start(bf16[8,1024]{1,0:T(8,128)(2,1)} %param.8) | copy-start | bytes 49156
  17.1 15.1 %all-to-all-start = ((bf16[512,4,128]{0,2,1:T(8,128)(2,1)}), bf16[512,4,128]{0,2,1:T(8,128)(2,1)S(1)}, u32[]{:S(2)}, u32[]{:S(2)}) async-start(bf16[512,4,128]{0,2,1:T(8,128)(2,1)} %bitcast), calls=%async_computation | async-start | bytes 1048576 | tf_op jit(solution)/shard_map/all_to_all | solution.py:53
  32.2 32.3 %all-to-all-start.1 = ((bf16[512,4,128]{0,2,1:T(8,128)(2,1)}), bf16[512,4,128]{0,2,1:T(8,128)(2,1)S(1)}, u32[]{:S(2)}, u32[]{:S(2)}) async-start(bf16[512,4,128]{0,2,1:T(8,128)(2,1)} %bitcast.2), calls=%async_computation.1 | async-start | bytes 1048576 | tf_op jit(solution)/shard_map/all_to_all | solution.py:52
  37.0 220.4 %all-reduce.2.cloned.1.call-start = ((), (), s32[]{:S(2)}) async-start(), calls=%async_computation.3 | async-start | bytes 1048576 | tf_op jit(solution)/shard_map/psum | solution.py:61
  156.0 124.0 %reduce-scatter.2.cloned.1.call-start = ((), (), s32[]{:S(2)}) async-start(), calls=%async_computation.4 | async-start | bytes 163840 | tf_op jit(solution)/shard_map/reduce_scatter | solution.py:64
Sparse Core Ops, SparseCore 0:
  156.1 101.2 all-reduce.1
  259.8 20.1 reduce-scatter.1
where the time goes:
time: 287 us
  blocking collectives  156 us (54%)
  waiting for transfers between devices  59 us (21%)
  matrix products  37.6 us (13%)
  between operations  13.5 us (5%)
  other arithmetic  10.5 us (4%)
  starting transfers between devices  9.38 us (3%)
    pmax x1, blocking collectives, shards(): global_max = lax.pmax(maxima, 'seq')  66.3 us
    psum x1, blocking collectives, shards(): lax.psum((totals * factor).astype(jnp.bfloat16), 'seq').astype(jnp.float32)  62.8 us
    psum x1, waiting for transfers between devices, shards(): lax.psum(scale_rows(partial_value, factor).astype(jnp.bfloat16), 'seq')  38.6 us
    all_gather x1, blocking collectives, shards(): queries_all = lax.all_gather(queries, 'seq', axis=0, tiled=True)  26.5 us
    reduce_scatter x1, waiting for transfers between devices, shards(): lax.psum_scatter(jnp.dot(attended, w_out, preferred_element_type=jnp.floa...  20.4 us
    dot_general x1, matrix products, shards(): jnp.dot(vision, w_value, preferred_element_type=jnp.float32)  10.6 us
    dot_general x1, matrix products, shards(): jnp.dot(vision, w_key, preferred_element_type=jnp.float32)  10.5 us
    reduce_sum x1, other arithmetic, attend(): totals = jnp.sum(powers, axis=-1)  8.48 us
  transfers between devices with their start and end apart: 4, of which 2 were waited for; matrix products, arithmetic and copies ran while one was open for 4% of the time, Pallas kernels for 0%

commit v1 on v0

v1 whole, which is shorter than its diff:
```python
import math

import jax
import jax.numpy as jnp
from jax import lax
from jax.experimental import pallas as pl
from jax.experimental.pallas import tpu as pltpu
from jax.sharding import Mesh, PartitionSpec as P

HD = 128
HEADS = 8
RPD = 8
PEERS = 16
ROWS = PEERS * RPD
TOK = 512
BLK = HEADS + 1
EXP2_SCALE = HD ** -0.5 * math.log2(math.e)
VMEM = pl.BlockSpec(memory_space=pltpu.VMEM)
ANY = pl.BlockSpec(memory_space=pl.ANY)
SMEM = pl.BlockSpec(memory_space=pltpu.SMEM)
YZ = ("y", "z")
CHUNKS = (768,) * 10
AHEAD = 2


def project_kernel(x, wk, wv, ko, vo, xb, wkb, wvb, acck, accv, sems):
    offsets = [sum(CHUNKS[:i]) for i in range(len(CHUNKS))]
    copies = []
    for i, (at, size) in enumerate(zip(offsets, CHUNKS)):
        part = pl.ds(at, size)
        copies.append(
            [
                pltpu.make_async_copy(x.at[:, part], xb.at[:, part], sems.at[0, i]),
                pltpu.make_async_copy(wk.at[part, :], wkb.at[part, :], sems.at[1, i]),
                pltpu.make_async_copy(wv.at[part, :], wvb.at[part, :], sems.at[2, i]),
            ]
        )
    for i in range(AHEAD):
        for copy in copies[i]:
            copy.start()
    last = len(CHUNKS) - 1
    for i, (at, size) in enumerate(zip(offsets, CHUNKS)):
        for copy in copies[i]:
            copy.wait()
        if i + AHEAD <= last:
            for copy in copies[i + AHEAD]:
                copy.start()
        for w, acc, out in ((wkb, acck, ko), (wvb, accv, vo)):
            part = jnp.dot(
                xb[:, at : at + size], w[at : at + size, :], preferred_element_type=jnp.float32
            )
            if i > 0:
                part = acc[...] + part
            if i < last:
                acc[...] = part
            else:
                for h in range(4):
                    out[h] = part[:, h * HD : (h + 1) * HD].astype(jnp.bfloat16)


def project(vision, w_key, w_value):
    rows, width = vision.shape
    cols = w_key.shape[1]
    out = jax.ShapeDtypeStruct((4, rows, HD), jnp.bfloat16)
    return pl.pallas_call(
        project_kernel,
        in_specs=[ANY] * 3,
        out_specs=[VMEM] * 2,
        out_shape=[out] * 2,
        scratch_shapes=[
            pltpu.VMEM((rows, width), jnp.bfloat16),
            pltpu.VMEM((width, cols), jnp.bfloat16),
            pltpu.VMEM((width, cols), jnp.bfloat16),
            pltpu.VMEM((rows, cols), jnp.float32),
            pltpu.VMEM((rows, cols), jnp.float32),
            pltpu.SemaphoreType.DMA((3, len(CHUNKS))),
        ],
        name="project",
    )(vision, w_key, w_value)


def attend_kernel(q, k1, v1, k2, v2, out):
    tokens = k1.shape[0]
    sub = lax.broadcasted_iota(jnp.int32, (ROWS, HD), 0) % RPD
    lane = lax.broadcasted_iota(jnp.int32, (ROWS, HD), 1)
    stats = jnp.zeros((ROWS, HD), jnp.float32)
    contract = (((1,), (1,)), ((), ()))
    ones = jnp.ones((tokens, HD), jnp.bfloat16)
    for h in range(HEADS):
        qh = q[:, h * HD : (h + 1) * HD]
        s1 = lax.dot_general(qh, k1[...], contract, preferred_element_type=jnp.float32)
        s2 = lax.dot_general(qh, k2[...], contract, preferred_element_type=jnp.float32)
        top = jnp.maximum(
            jnp.max(s1, axis=1, keepdims=True), jnp.max(s2, axis=1, keepdims=True)
        )
        p1 = jnp.exp2((s1 - top) * EXP2_SCALE).astype(jnp.bfloat16)
        p2 = jnp.exp2((s2 - top) * EXP2_SCALE).astype(jnp.bfloat16)
        acc = jnp.dot(
            p1, jnp.concatenate([v1[...], ones], axis=1), preferred_element_type=jnp.float32
        ) + jnp.dot(
            p2, jnp.concatenate([v2[...], ones], axis=1), preferred_element_type=jnp.float32
        )
        out[:, h] = acc[:, :HD].reshape(PEERS, RPD, HD).astype(jnp.bfloat16)
        stats = jnp.where(lane == h * RPD + sub, top, stats)
        stats = jnp.where(lane == HD // 2 + h * RPD + sub, acc[:, HD:], stats)
    mine = jnp.sum(stats.reshape(PEERS, RPD, HD), axis=1, keepdims=True)
    high = mine.astype(jnp.bfloat16).astype(jnp.float32)
    rest = mine - high
    mid = rest.astype(jnp.bfloat16).astype(jnp.float32)
    low = rest - mid
    place = lax.broadcasted_iota(jnp.int32, (PEERS, RPD, HD), 1)
    tile = jnp.where(
        place == 0, high, jnp.where(place == 1, mid, jnp.where(place == 2, low, 0.0))
    )
    out[:, HEADS] = tile.astype(jnp.bfloat16)


def attend(q, k1, v1, k2, v2):
    return pl.pallas_call(
        attend_kernel,
        in_specs=[VMEM] * 5,
        out_specs=VMEM,
        out_shape=jax.ShapeDtypeStruct((PEERS, BLK, RPD, HD), jnp.bfloat16),
        name="attend",
    )(q, k1, v1, k2, v2)


def combine_kernel(parts, out):
    half = HD // 2
    tile = parts[:, HEADS].astype(jnp.float32)
    stats = jnp.sum(tile, axis=1)
    maxima = stats[:, :half]
    sums = stats[:, half:]
    top = jnp.max(maxima, axis=0, keepdims=True)
    factor = jnp.exp2((maxima - top) * EXP2_SCALE)
    denom = jnp.sum(factor * sums, axis=0, keepdims=True)
    weight = (factor / denom).T
    total = jnp.zeros((HEADS * RPD, HD), jnp.float32)
    for s in range(PEERS):
        block = parts[s, :HEADS].astype(jnp.float32).reshape(HEADS * RPD, HD)
        total = total + block * weight[:, s : s + 1]
    total = total.reshape(HEADS, RPD, HD)
    row = jnp.concatenate([total[h] for h in range(HEADS)], axis=1).astype(jnp.bfloat16)
    for s in range(PEERS):
        out[s] = row


def combine(parts):
    return pl.pallas_call(
        combine_kernel,
        in_specs=[VMEM],
        out_specs=VMEM,
        out_shape=jax.ShapeDtypeStruct((PEERS, RPD, HEADS * HD), jnp.bfloat16),
        name="combine",
    )(parts)


def mix_kernel(core, own, other, w, out):
    cols = w.shape[1]
    mine = jnp.dot(own[...], w[...], preferred_element_type=jnp.float32)
    theirs = jnp.dot(other[...], w[...], preferred_element_type=jnp.float32)
    mine = mine.reshape(PEERS, 1, RPD, cols)
    theirs = theirs.reshape(PEERS, 1, RPD, cols)
    first = core[0] == 0
    pair = jnp.concatenate(
        [jnp.where(first, mine, theirs), jnp.where(first, theirs, mine)], axis=1
    )
    out[...] = pair.reshape(2 * ROWS, cols).astype(jnp.bfloat16)


def mix(core, own, other, w):
    return pl.pallas_call(
        mix_kernel,
        in_specs=[SMEM, VMEM, VMEM, VMEM],
        out_specs=VMEM,
        out_shape=jax.ShapeDtypeStruct((2 * ROWS, w.shape[1]), jnp.bfloat16),
        name="mix",
    )(core, own, other, w)


def swap_cores(x):
    return lax.ppermute(x, "core", [(0, 1), (1, 0)])


def exchange(x, axes):
    return lax.all_to_all(x, axes, split_axis=0, concat_axis=0, tiled=True)


def shards(vision, w_key, w_value, queries, w_out):
    rows = exchange(jnp.tile(queries, (PEERS, 1)), YZ)
    keys, values = project(vision, w_key, w_value)
    k1 = exchange(keys, "head").reshape(-1, HD)
    v1 = exchange(values, "head").reshape(-1, HD)
    k2 = swap_cores(k1)
    v2 = swap_cores(v1)
    parts = exchange(attend(rows, k1, v1, k2, v2), YZ)
    own = exchange(combine(parts), YZ).reshape(ROWS, HEADS * HD)
    other = swap_cores(own)
    core = lax.axis_index("core").astype(jnp.int32).reshape(1)
    partial = mix(core, own, other, w_out)
    shares = exchange(partial, "head").reshape(4, -1, partial.shape[1])
    return jnp.sum(shares.astype(jnp.float32), axis=0).astype(jnp.bfloat16)


def solution(mesh):
    fine = Mesh(mesh.devices.reshape(4, 4, 2, 4), ("y", "z", "core", "head"))
    seq = ("y", "z", "core")
    placed = (P(seq + ("head",), None), P(), P(), P(seq, "head"), P("head", seq))
    return jax.shard_map(
        shards, mesh=fine, in_specs=placed, out_specs=P("head", seq), check_vma=False
    )
```

time: 287 us -> 107 us (0.37)
  blocking collectives: 156 us -> 65.3 us
  waiting for transfers between devices: 59 us -> 10 us
  matrix products: 37.6 us -> 0 us
  Pallas kernels: 0 us -> 25.3 us
  between operations: 13.5 us -> 0.07 us
  other arithmetic: 10.5 us -> 0.64 us
  starting transfers between devices: 9.38 us -> 3.56 us
    pmax x1 -> x0, blocking collectives: 66.3 us -> none  [shards(): global_max = lax.pmax(maxima, 'seq')]
    all_to_all x0 -> x5, blocking collectives: none -> 65.3 us  [exchange(): return lax.all_to_all(x, axes, split_axis=0, concat_axis=0, tiled=True)]
    psum x1 -> x0, blocking collectives: 62.8 us -> none  [shards(): lax.psum((totals * factor).astype(jnp.bfloat16), 'seq').astype(jnp.float32)]
    psum x1 -> x0, waiting for transfers between devices: 38.6 us -> none  [shards(): lax.psum(scale_rows(partial_value, factor).astype(jnp.bfloat16), 'seq')]
    dot_general x5 -> x0, matrix products: 37.6 us -> none  [the longest x1 10.6 us: shards(): jnp.dot(vision, w_value, preferred_element_type=jnp.float32)]
    all_gather x1 -> x0, blocking collectives: 26.5 us -> none  [shards(): queries_all = lax.all_gather(queries, 'seq', axis=0, tiled=True)]
    pallas_call x0 -> x4, Pallas kernels: none -> 25.3 us  [the longest x1 11.7 us: project(): pl.pallas_call(project_kernel, in_specs=[ANY] * 3, out_specs=[VMEM] * 2,...]
    reduce_scatter x1 -> x0, waiting for transfers between devices: 20.4 us -> none  [shards(): lax.psum_scatter(jnp.dot(attended, w_out, preferred_element_type=jnp.floa...]
  transfers between devices with their start and end apart: 4 -> 4, of which waited for: 2 -> 2; matrix products, arithmetic and copies ran while one was open for 4% -> 0% of each run, Pallas kernels for 0% -> 0%
where the time goes in v1:
time: 107 us
  blocking collectives  65.3 us (61%)
  Pallas kernels  25.3 us (24%)
  waiting for transfers between devices  10 us (9%)
  starting transfers between devices  3.56 us (3%)
  local copies, waits for them, and re-layouts  1.72 us (2%)
    all_to_all x5, blocking collectives, exchange(): return lax.all_to_all(x, axes, split_axis=0, concat_axis=0, tiled=True)  65.3 us
    pallas_call x1, Pallas kernels, project(): pl.pallas_call(project_kernel, in_specs=[ANY] * 3, out_specs=[VMEM] * 2,...  11.7 us
    pallas_call x1, Pallas kernels, attend(): pl.pallas_call(attend_kernel, in_specs=[VMEM] * 5, out_specs=VMEM, out_sh...  9.4 us
    all_to_all x1, waiting for transfers between devices, exchange(): return lax.all_to_all(x, axes, split_axis=0, concat_axis=0, tiled=True)  8.49 us
    all_to_all x1, starting transfers between devices, exchange(): return lax.all_to_all(x, axes, split_axis=0, concat_axis=0, tiled=True)  3.47 us
    pallas_call x1, Pallas kernels, mix(): pl.pallas_call(mix_kernel, in_specs=[SMEM, VMEM, VMEM, VMEM], out_specs=V...  2.16 us
  transfers between devices with their start and end apart: 4, of which 2 were waited for; matrix products, arithmetic and copies ran while one was open for 0% of the time, Pallas kernels for 0%

profile of v1, /device:TPU:0, one launch (start us, length us, event | category | flops | bytes accessed | tf_op | source)
XLA Modules:
  0.0 106.6 jit_solution(16910932290315473836)
XLA Ops:
  0.0 0.0 copy-start.6
  0.0 11.7 %project.1 = (bf16[4,512,128]{2,1,0:T(8,128)(2,1)}, bf16[4,512,128]{2,1,0:T(8,128)(2,1)}) custom-call(bf16[512,7680]{1,0:T(8,128)(2,1)} %x.1, bf16[7680,512]{1,0:T(8,128)(2,1)} %wk.1, bf16[7680,512]{1,0:T(8,128)(2,1)} %wv.1), custom_call_target="tpu_custom_call" | custom-call | tf_op jit(solution)/shard_map/project/pallas_call | solution.py:65
  11.7 13.9 %all_to_all.37 = bf16[4,512,128]{2,1,0:T(8,128)(2,1)S(1)} all-to-all(bf16[4,512,128]{2,1,0:T(8,128)(2,1)} %get-tuple-element.7), channel_id=1, replica_groups=mesh['y'=4,'z'=4,'core'=2,'head'=4] {'head'}, dimensions={0} | all-to-all | bytes 1048576 | tf_op jit(solution)/shard_map/all_to_all | solution.py:186
  25.6 0.0 copy-start
  25.6 3.5 %all-to-all-start.2 = ((bf16[4,512,128]{2,1,0:T(8,128)(2,1)}), bf16[4,512,128]{2,1,0:T(8,128)(2,1)S(1)}, u32[]{:S(2)}, u32[]{:S(2)}) async-start(bf16[4,512,128]{2,1,0:T(8,128)(2,1)} %get-tuple-element.8), calls=%async_computation.2 | async-start | bytes 1048576 | tf_op jit(solution)/shard_map/all_to_all | solution.py:186
  29.0 0.1 collective-permute-start
  29.1 8.5 %all-to-all-done.2 = bf16[4,512,128]{2,1,0:T(8,128)(2,1)S(1)} async-done(((bf16[4,512,128]{2,1,0:T(8,128)(2,1)}), bf16[4,512,128]{2,1,0:T(8,128)(2,1)S(1)}, u32[]{:S(2)}, u32[]{:S(2)}) %all-to-all-start.2) | async-done | bytes 524320 | tf_op jit(solution)/shard_map/all_to_all | solution.py:186
  37.6 0.0 copy-start.1
  37.6 0.0 collective-permute-start.1
  37.6 0.0 copy-done.6
  37.7 17.1 %all_to_all.38 = bf16[16,8,1024]{2,1,0:T(8,128)(2,1)} all-to-all(bf16[16,8,1024]{2,1,0:T(8,128)(2,1)S(1)} %tile.2), channel_id=1, replica_groups=mesh['y'=4,'z'=4,'core'=2,'head'=4] {'y','z'}, dimensions={0} | all-to-all | bytes 524288 | tf_op jit(solution)/shard_map/all_to_all | solution.py:186
  54.8 0.0 collective-permute-done.k2
  54.8 0.0 copy-start.3
  54.8 0.0 collective-permute-done.1.v2
  54.8 0.0 copy-start.4
  54.8 0.0 copy-done
  54.8 0.0 copy-done.1
  54.8 0.8 copy-done.3
  55.6 0.2 copy-done.4
  55.8 9.4 %attend.1 = bf16[16,9,8,128]{3,2,1,0:T(8,128)(2,1)} custom-call(bf16[128,1024]{1,0:T(8,128)(2,1)} %bitcast.12, bf16[2048,128]{1,0:T(8,128)(2,1)} %bitcast.7, bf16[2048,128]{1,0:T(8,128)(2,1)} %bitcast.9, bf16[2048,128]{1,0:T(8,128)(2,1)} %copy-done.3, bf16[2048,128]{1,0:T(8,128)(2,1)} %copy-done.4), custom_call_target="tpu_custom_call" | custom-call | tf_op jit(solution)/shard_map/attend/pallas_call | solution.py:119
  65.2 12.9 %all_to_all.39.parts = bf16[16,9,8,128]{3,2,1,0:T(8,128)(2,1)} all-to-all(bf16[16,9,8,128]{3,2,1,0:T(8,128)(2,1)} %attend.1), channel_id=1, replica_groups=mesh['y'=4,'z'=4,'core'=2,'head'=4] {'y','z'}, dimensions={0} | all-to-all | bytes 589824 | tf_op jit(solution)/shard_map/all_to_all | solution.py:186
  78.1 2.1 %combine.1 = bf16[16,8,1024]{2,1,0:T(8,128)(2,1)} custom-call(bf16[16,9,8,128]{3,2,1,0:T(8,128)(2,1)} %all_to_all.39.parts), custom_call_target="tpu_custom_call" | custom-call | tf_op jit(solution)/shard_map/combine/pallas_call | solution.py:149
  80.2 12.1 %all_to_all.40 = bf16[16,8,1024]{2,1,0:T(8,128)(2,1)S(1)} all-to-all(bf16[16,8,1024]{2,1,0:T(8,128)(2,1)} %combine.1), channel_id=1, replica_groups=mesh['y'=4,'z'=4,'core'=2,'head'=4] {'y','z'}, dimensions={0} | all-to-all | bytes 524288 | tf_op jit(solution)/shard_map/all_to_all | solution.py:186
  92.3 0.0 copy-start.2
  92.3 0.0 collective-permute-start.2
  92.3 1.5 %collective-permute-done.2.other = bf16[128,1024]{1,0:T(8,128)(2,1)S(1)} collective-permute-done((bf16[128,1024]{1,0:T(8,128)(2,1)S(1)}, bf16[128,1024]{1,0:T(8,128)(2,1)S(1)}, u32[]{:S(2)}, u32[]{:S(2)}) %collective-permute-start.2) | collective-permute-done | bytes 262176 | tf_op jit(solution)/shard_map/ppermute | solution.py:182
  93.9 0.0 copy-start.5
  93.9 0.0 copy-done.2
  93.9 0.7 copy-done.5
  94.6 2.2 %mix.1 = bf16[256,256]{1,0:T(8,128)(2,1)} custom-call(s32[1]{0:T(128)} %bitcast.core, bf16[128,1024]{1,0:T(8,128)(2,1)} %bitcast.11, bf16[128,1024]{1,0:T(8,128)(2,1)} %copy-done.5, bf16[1024,256]{1,0:T(8,128)(2,1)} %w.1), custom_call_target="tpu_custom_call" | custom-call | tf_op jit(solution)/shard_map/mix/pallas_call | solution.py:172
  96.7 9.3 %all_to_all.41 = bf16[4,64,256]{2,1,0:T(8,128)(2,1)S(1)} all-to-all(bf16[4,64,256]{2,1,0:T(8,128)(2,1)} %bitcast.13), channel_id=1, replica_groups=mesh['y'=4,'z'=4,'core'=2,'head'=4] {'head'}, dimensions={0} | all-to-all | bytes 262144 | tf_op jit(solution)/shard_map/all_to_all | solution.py:186
  106.0 0.6 reduce_sum.12
  (1 shorter events, 0.0 us)
Async XLA Ops:
  0.0 37.6 %copy-start.6 = (bf16[8,1024]{1,0:T(8,128)(2,1)S(1)}, bf16[8,1024]{1,0:T(8,128)(2,1)}, u32[]{:S(2)}) copy-start(bf16[8,1024]{1,0:T(8,128)(2,1)} %param.8) | copy-start | bytes 49156
  25.6 29.2 %copy-start = (bf16[4,512,128]{2,1,0:T(8,128)(2,1)}, bf16[4,512,128]{2,1,0:T(8,128)(2,1)S(1)}, u32[]{:S(2)}) copy-start(bf16[4,512,128]{2,1,0:T(8,128)(2,1)S(1)} %all_to_all.37) | copy-start | bytes 1572868
  25.6 12.1 %all-to-all-start.2 = ((bf16[4,512,128]{2,1,0:T(8,128)(2,1)}), bf16[4,512,128]{2,1,0:T(8,128)(2,1)S(1)}, u32[]{:S(2)}, u32[]{:S(2)}) async-start(bf16[4,512,128]{2,1,0:T(8,128)(2,1)} %get-tuple-element.8), calls=%async_computation.2 | async-start | bytes 1048576 | tf_op jit(solution)/shard_map/all_to_all | solution.py:186
  29.0 25.7 %collective-permute-start = (bf16[2048,128]{1,0:T(8,128)(2,1)S(1)}, bf16[2048,128]{1,0:T(8,128)(2,1)S(1)}, u32[]{:S(2)}, u32[]{:S(2)}) collective-permute-start(bf16[2048,128]{1,0:T(8,128)(2,1)S(1)} %bitcast.6), channel_id=1, source_target_pairs={{0,4},{4,0},{1,5},{5,1},{2,6},{6,2},{3,7},{7,3},{8,12},{12,8},{9,1... | collective-permute-start | bytes 1572872 | tf_op jit(solution)/shard_map/ppermute | solution.py:182
  37.6 17.2 %copy-start.1 = (bf16[4,512,128]{2,1,0:T(8,128)(2,1)}, bf16[4,512,128]{2,1,0:T(8,128)(2,1)S(1)}, u32[]{:S(2)}) copy-start(bf16[4,512,128]{2,1,0:T(8,128)(2,1)S(1)} %all-to-all-done.2) | copy-start | bytes 1572868
  37.6 17.2 %collective-permute-start.1 = (bf16[2048,128]{1,0:T(8,128)(2,1)S(1)}, bf16[2048,128]{1,0:T(8,128)(2,1)S(1)}, u32[]{:S(2)}, u32[]{:S(2)}) collective-permute-start(bf16[2048,128]{1,0:T(8,128)(2,1)S(1)} %bitcast.8), channel_id=1, source_target_pairs={{0,4},{4,0},{1,5},{5,1},{2,6},{6,2},{3,7},{7,3},{8,12},{12,8},{9,1... | collective-permute-start | bytes 1572872 | tf_op jit(solution)/shard_map/ppermute | solution.py:182
  54.8 0.8 copy-start.3
  54.8 1.0 copy-start.4
  92.3 1.5 %copy-start.2 = (bf16[16,8,1024]{2,1,0:T(8,128)(2,1)}, bf16[16,8,1024]{2,1,0:T(8,128)(2,1)S(1)}, u32[]{:S(2)}) copy-start(bf16[16,8,1024]{2,1,0:T(8,128)(2,1)S(1)} %all_to_all.40) | copy-start | bytes 786436
  92.3 1.5 %collective-permute-start.2 = (bf16[128,1024]{1,0:T(8,128)(2,1)S(1)}, bf16[128,1024]{1,0:T(8,128)(2,1)S(1)}, u32[]{:S(2)}, u32[]{:S(2)}) collective-permute-start(bf16[128,1024]{1,0:T(8,128)(2,1)S(1)} %bitcast.10), channel_id=1, source_target_pairs={{0,4},{4,0},{1,5},{5,1},{2,6},{6,2},{3,7},{7,3},{8,12},{12,8},{9,1... | collective-permute-start | bytes 786440 | tf_op jit(solution)/shard_map/ppermute | solution.py:182
  93.9 0.7 copy-start.5

commit v2 on v1

v2 whole, which is shorter than its diff:
```python
import math

import jax
import jax.numpy as jnp
from jax import lax
from jax.experimental import pallas as pl
from jax.experimental.pallas import tpu as pltpu
from jax.sharding import Mesh, PartitionSpec as P


HD = 128
GROUPS = 4
HEADS = 8
RPD = 8
YZ_SIZE = 16
PEERS = YZ_SIZE * GROUPS
ROWS = YZ_SIZE * RPD
BLK = HEADS + 1
STACK = 2
EXP2_SCALE = HD ** -0.5 * math.log2(math.e)
VMEM = pl.BlockSpec(memory_space=pltpu.VMEM)
HBM = pl.BlockSpec(memory_space=pltpu.HBM)
SMEM = pl.BlockSpec(memory_space=pltpu.SMEM)
YZ = ("y", "z")
YZX = ("y", "z", "head")
CHUNKS = (768,) * 10
AHEAD = 3


def limit(mib):
    return pltpu.CompilerParams(vmem_limit_bytes=mib * 1024 * 1024)


def project_kernel(x, wk, wv, out, xb, wkb, wvb, acc, sems):
    offsets = [sum(CHUNKS[:i]) for i in range(len(CHUNKS))]
    copies = []
    for i, (at, size) in enumerate(zip(offsets, CHUNKS)):
        part = pl.ds(at, size)
        copies.append(
            [
                pltpu.make_async_copy(x.at[:, part], xb.at[:, part], sems.at[0, i]),
                pltpu.make_async_copy(wk.at[part, :], wkb.at[part, :], sems.at[1, i]),
                pltpu.make_async_copy(wv.at[part, :], wvb.at[part, :], sems.at[2, i]),
            ]
        )
    for i in range(AHEAD):
        for copy in copies[i]:
            copy.start()
    last = len(CHUNKS) - 1
    for i, (at, size) in enumerate(zip(offsets, CHUNKS)):
        for copy in copies[i]:
            copy.wait()
        if i + AHEAD <= last:
            for copy in copies[i + AHEAD]:
                copy.start()
        for j, w in enumerate((wkb, wvb)):
            part = jnp.dot(
                xb[:, at : at + size], w[at : at + size, :], preferred_element_type=jnp.float32
            )
            if i > 0:
                part = acc[j] + part
            if i < last:
                acc[j] = part
            else:
                for g in range(GROUPS):
                    out[g, j] = part[:, g * HD : (g + 1) * HD].astype(jnp.bfloat16)


def project(vision, w_key, w_value):
    rows, width = vision.shape
    cols = w_key.shape[1]
    return pl.pallas_call(
        project_kernel,
        in_specs=[HBM] * 3,
        out_specs=VMEM,
        out_shape=jax.ShapeDtypeStruct((GROUPS, 2, rows, HD), jnp.bfloat16),
        scratch_shapes=[
            pltpu.VMEM((rows, width), jnp.bfloat16),
            pltpu.VMEM((width, cols), jnp.bfloat16),
            pltpu.VMEM((width, cols), jnp.bfloat16),
            pltpu.VMEM((2, rows, cols), jnp.float32),
            pltpu.SemaphoreType.DMA((3, len(CHUNKS))),
        ],
        compiler_params=limit(56),
        name="project",
    )(vision, w_key, w_value)


def split_stats(stats):
    mine = jnp.sum(stats.reshape(YZ_SIZE, RPD, HD), axis=1, keepdims=True)
    high = mine.astype(jnp.bfloat16).astype(jnp.float32)
    rest = mine - high
    mid = rest.astype(jnp.bfloat16).astype(jnp.float32)
    low = rest - mid
    place = lax.broadcasted_iota(jnp.int32, (YZ_SIZE, RPD, HD), 1)
    tile = jnp.where(
        place == 0, high, jnp.where(place == 1, mid, jnp.where(place == 2, low, 0.0))
    )
    return tile.astype(jnp.bfloat16)


def peer_of(tile, group):
    block, part = divmod(tile, GROUPS)
    slot = (group - block) % GROUPS
    return (part * GROUPS + slot) * GROUPS + block


def attend_kernel(q, kv1, kv2, out):
    tokens = kv1.shape[2]
    sub = lax.broadcasted_iota(jnp.int32, (ROWS, HD), 0) % RPD
    lane = lax.broadcasted_iota(jnp.int32, (ROWS, HD), 1)
    contract = (((1,), (1,)), ((), ()))
    ones = jnp.ones((tokens, HD), jnp.bfloat16)
    for g in range(GROUPS):
        stats = jnp.zeros((ROWS, HD), jnp.float32)
        v1 = jnp.concatenate([kv1[g, 1], ones], axis=1)
        v2 = jnp.concatenate([kv2[g, 1], ones], axis=1)
        for first in range(0, HEADS, STACK):
            qs = [
                q[:, g, :, h * HD : (h + 1) * HD].reshape(ROWS, HD)
                for h in range(first, first + STACK)
            ]
            qs = jnp.concatenate(qs, axis=0)
            s1 = lax.dot_general(qs, kv1[g, 0], contract, preferred_element_type=jnp.float32)
            s2 = lax.dot_general(qs, kv2[g, 0], contract, preferred_element_type=jnp.float32)
            top = jnp.max(jnp.maximum(s1, s2), axis=1, keepdims=True)
            p1 = jnp.exp2((s1 - top) * EXP2_SCALE).astype(jnp.bfloat16)
            p2 = jnp.exp2((s2 - top) * EXP2_SCALE).astype(jnp.bfloat16)
            acc = jnp.dot(p1, v1, preferred_element_type=jnp.float32) + jnp.dot(
                p2, v2, preferred_element_type=jnp.float32
            )
            for k in range(STACK):
                h = first + k
                mine = acc[k * ROWS : (k + 1) * ROWS]
                for t in range(YZ_SIZE):
                    out[peer_of(t, g), h] = mine[t * RPD : (t + 1) * RPD, :HD].astype(
                        jnp.bfloat16
                    )
                stats = jnp.where(
                    lane == h * RPD + sub, top[k * ROWS : (k + 1) * ROWS], stats
                )
                stats = jnp.where(lane == HD // 2 + h * RPD + sub, mine[:, HD:], stats)
        tiles = split_stats(stats)
        for t in range(YZ_SIZE):
            out[peer_of(t, g), HEADS] = tiles[t]


def attend(q, kv1, kv2):
    return pl.pallas_call(
        attend_kernel,
        in_specs=[VMEM] * 3,
        out_specs=VMEM,
        out_shape=jax.ShapeDtypeStruct((PEERS, BLK, RPD, HD), jnp.bfloat16),
        compiler_params=limit(32),
        name="attend",
    )(q, kv1, kv2)


def combine_kernel(parts, out):
    half = HD // 2
    tile = parts[:, HEADS].astype(jnp.float32)
    stats = jnp.sum(tile, axis=1)
    maxima = stats[:, :half]
    sums = stats[:, half:]
    top = jnp.max(maxima, axis=0, keepdims=True)
    factor = jnp.exp2((maxima - top) * EXP2_SCALE)
    denom = jnp.sum(factor * sums, axis=0, keepdims=True)
    weight = (factor / denom).T
    total = jnp.zeros((HEADS * RPD, HD), jnp.float32)
    for s in range(PEERS):
        block = parts[s, :HEADS].astype(jnp.float32).reshape(HEADS * RPD, HD)
        total = total + block * weight[:, s : s + 1]
    total = total.reshape(HEADS, RPD, HD)
    row = jnp.concatenate([total[h] for h in range(HEADS)], axis=1).astype(jnp.bfloat16)
    for s in range(YZ_SIZE):
        out[s] = row


def combine(parts):
    return pl.pallas_call(
        combine_kernel,
        in_specs=[VMEM],
        out_specs=VMEM,
        out_shape=jax.ShapeDtypeStruct((YZ_SIZE, RPD, HEADS * HD), jnp.bfloat16),
        compiler_params=limit(8),
        name="combine",
    )(parts)


def mix_kernel(core, own, other, w0, w1, w2, w3, out):
    cols = w0.shape[1]
    half = GROUPS * RPD
    total = jnp.zeros((2 * half, cols), jnp.float32)
    for slot, w in enumerate((w0, w1, w2, w3)):
        rows = jnp.concatenate(
            [own[:, slot].reshape(half, -1), other[:, slot].reshape(half, -1)], axis=0
        )
        total = total + jnp.dot(rows, w[...], preferred_element_type=jnp.float32)
    mine = total[:half].reshape(GROUPS, 1, RPD, cols)
    theirs = total[half:].reshape(GROUPS, 1, RPD, cols)
    first = core[0] == 0
    pair = jnp.concatenate(
        [jnp.where(first, mine, theirs), jnp.where(first, theirs, mine)], axis=1
    )
    out[...] = pair.reshape(2 * half, cols).astype(jnp.bfloat16)


def mix(core, own, other, shares):
    return pl.pallas_call(
        mix_kernel,
        in_specs=[SMEM] + [VMEM] * 6,
        out_specs=VMEM,
        out_shape=jax.ShapeDtypeStruct((2 * GROUPS * RPD, shares[0].shape[1]), jnp.bfloat16),
        compiler_params=limit(8),
        name="mix",
    )(core, own, other, *shares)


def swap_cores(x):
    return lax.ppermute(x, "core", [(0, 1), (1, 0)])


def exchange(x, axes):
    return lax.all_to_all(x, axes, split_axis=0, concat_axis=0, tiled=True)


def gather_share(w, ahead):
    return lax.ppermute(w, "head", [((i + ahead) % GROUPS, i) for i in range(GROUPS)])


def shards(vision, w_key, w_value, queries, w_out):
    copies = jnp.broadcast_to(queries[None], (PEERS,) + queries.shape)
    rows = exchange(copies, YZX).reshape(YZ_SIZE, GROUPS, RPD, -1)
    shares = [w_out] + [gather_share(w_out, k) for k in range(1, GROUPS)]
    kv1 = project(vision, w_key, w_value)
    kv2 = swap_cores(kv1)
    parts = exchange(attend(rows, kv1, kv2), YZX)
    own = exchange(combine(parts), YZ)
    other = swap_cores(own)
    core = lax.axis_index("core").astype(jnp.int32).reshape(1)
    shape = (GROUPS, GROUPS, RPD, -1)
    return mix(core, own.reshape(shape), other.reshape(shape), shares)


def solution(mesh):
    fine = Mesh(mesh.devices.reshape(4, 4, 2, 4), ("y", "z", "core", "head"))
    seq = ("y", "z", "core")
    placed = (P(seq + ("head",), None), P(), P(), P(seq, "head"), P("head", seq))
    return jax.shard_map(
        shards, mesh=fine, in_specs=placed, out_specs=P("head", seq), check_vma=False
    )
```

time: 107 us -> 102 us (0.953)
  blocking collectives: 65.3 us -> 42.7 us
  waiting for transfers between devices: 10 us -> 27.3 us
  starting transfers between devices: 3.56 us -> 9.2 us
  Pallas kernels: 25.3 us -> 20.2 us
    all_to_all x5 -> x2, blocking collectives: 65.3 us -> 42.7 us  [exchange(): return lax.all_to_all(x, axes, split_axis=0, concat_axis=0, tiled=True)]
    all_to_all x1, waiting for transfers between devices: 8.49 us -> 25.8 us  [exchange(): return lax.all_to_all(x, axes, split_axis=0, concat_axis=0, tiled=True)]
    ppermute x0 -> x3, starting transfers between devices: none -> 4.46 us  [gather_share(): lax.ppermute(w, 'head', [((i + ahead) % GROUPS, i) for i in range(GROUPS)])]
    pallas_call x3, Pallas kernels: 23.2 us -> 19.1 us  [the longest x1 11.6 us: project(): pl.pallas_call(project_kernel, in_specs=[HBM] * 3, out_specs=VMEM, out_sh...]
    all_to_all x1, starting transfers between devices: 3.47 us -> 4.66 us  [exchange(): return lax.all_to_all(x, axes, split_axis=0, concat_axis=0, tiled=True)]
  transfers between devices with their start and end apart: 4 -> 6, of which waited for: 2 -> 2; matrix products, arithmetic and copies ran while one was open for 0% -> 0% of each run, Pallas kernels for 0% -> 1%
where the time goes in v2:
time: 102 us; the launch traced here: 101 us
  blocking collectives  42.7 us (42%)
  waiting for transfers between devices  27.3 us (27%)
  Pallas kernels  20.2 us (20%)
  starting transfers between devices  9.2 us (9%)
  local copies, waits for them, and re-layouts  1.35 us (1%)
    all_to_all x2, blocking collectives, exchange(): return lax.all_to_all(x, axes, split_axis=0, concat_axis=0, tiled=True)  42.7 us
    all_to_all x1, waiting for transfers between devices, exchange(): return lax.all_to_all(x, axes, split_axis=0, concat_axis=0, tiled=True)  25.8 us
    pallas_call x1, Pallas kernels, project(): pl.pallas_call(project_kernel, in_specs=[HBM] * 3, out_specs=VMEM, out_sh...  11.6 us
    pallas_call x1, Pallas kernels, attend(): pl.pallas_call(attend_kernel, in_specs=[VMEM] * 3, out_specs=VMEM, out_sh...  6.41 us
    all_to_all x1, starting transfers between devices, exchange(): return lax.all_to_all(x, axes, split_axis=0, concat_axis=0, tiled=True)  4.66 us
    ppermute x3, starting transfers between devices, gather_share(): lax.ppermute(w, 'head', [((i + ahead) % GROUPS, i) for i in range(GROUPS)])  4.46 us
  transfers between devices with their start and end apart: 6, of which 2 were waited for; matrix products, arithmetic and copies ran while one was open for 0% of the time, Pallas kernels for 1%

profile of v2, /device:TPU:0, one launch (start us, length us, event | category | flops | bytes accessed | tf_op | source)
XLA Modules:
  0.0 100.8 jit_solution(16561767099456644756)
XLA Ops:
  0.0 0.0 copy-start.2
  0.0 11.6 %project.1.kv1 = bf16[4,2,512,128]{3,2,1,0:T(8,128)(2,1)} custom-call(bf16[512,7680]{1,0:T(8,128)(2,1)} %x.1, bf16[7680,512]{1,0:T(8,128)(2,1)} %wk.1, bf16[7680,512]{1,0:T(8,128)(2,1)} %wv.1), custom_call_target="tpu_custom_call" | custom-call | tf_op jit(solution)/shard_map/project/pallas_call | solution.py:72
  11.6 0.0 copy-start.1
  11.7 0.1 collective-permute-start
  11.7 0.0 copy-done.2
  11.8 0.1 broadcast_in_dim.2
  11.9 30.9 %all_to_all.15 = bf16[64,8,1024]{2,1,0:T(8,128)(2,1)S(1)} all-to-all(bf16[64,8,1024]{2,1,0:T(8,128)(2,1)S(1)} %broadcast_in_dim.2), channel_id=1, replica_groups=mesh['y'=4,'z'=4,'core'=2,'head'=4] {'y','z','head'}, dimensions={0} | all-to-all | bytes 2097152 | tf_op jit(solution)/shard_map/all_to_all | solution.py:224
  42.8 0.0 collective-permute-done.kv2
  42.8 0.0 copy-start
  42.8 1.2 %copy-done = bf16[4,2,512,128]{3,2,1,0:T(8,128)(2,1)S(1)} copy-done((bf16[4,2,512,128]{3,2,1,0:T(8,128)(2,1)S(1)}, bf16[4,2,512,128]{3,2,1,0:T(8,128)(2,1)}, u32[]{:S(2)}) %copy-start) | copy-done | bytes 1048600
  44.0 6.4 %attend.1 = bf16[64,9,8,128]{3,2,1,0:T(8,128)(2,1)} custom-call(bf16[16,4,8,1024]{3,2,1,0:T(8,128)(2,1)S(1)} %bitcast.4, bf16[4,2,512,128]{3,2,1,0:T(8,128)(2,1)S(1)} %copy-done, bf16[4,2,512,128]{3,2,1,0:T(8,128)(2,1)S(1)} %collective-permute-done.kv2), custom_call_target="tpu_custom_call" | custom-call | tf_op jit(solution)/shard_map/attend/pallas_call | solution.py:149
  50.4 4.7 %all-to-all-start.1 = ((bf16[64,9,8,128]{3,2,1,0:T(8,128)(2,1)}), bf16[64,9,8,128]{3,2,1,0:T(8,128)(2,1)S(1)}, u32[]{:S(2)}, u32[]{:S(2)}) async-start(bf16[64,9,8,128]{3,2,1,0:T(8,128)(2,1)} %attend.1), calls=%async_computation.1 | async-start | bytes 2359296 | tf_op jit(solution)/shard_map/all_to_all | solution.py:224
  55.1 0.0 copy-done.1
  55.1 2.8 %collective-permute-start.2 = (bf16[1024,256]{1,0:T(8,128)(2,1)S(1)}, bf16[1024,256]{1,0:T(8,128)(2,1)S(1)}, u32[]{:S(2)}, u32[]{:S(2)}) collective-permute-start(bf16[1024,256]{1,0:T(8,128)(2,1)S(1)} %copy-done.1), channel_id=1, source_target_pairs={{1,0},{2,1},{3,2},{0,3},{5,4},{6,5},{7,6},{4,7},{9,8},{10,9},{11,1... | collective-permute-start | bytes 1572872 | tf_op jit(solution)/shard_map/ppermute | solution.py:228
  57.9 0.8 collective-permute-start.3
  58.7 0.9 collective-permute-start.4
  59.6 25.8 %all-to-all-done.1.parts = bf16[64,9,8,128]{3,2,1,0:T(8,128)(2,1)S(1)} async-done(((bf16[64,9,8,128]{3,2,1,0:T(8,128)(2,1)}), bf16[64,9,8,128]{3,2,1,0:T(8,128)(2,1)S(1)}, u32[]{:S(2)}, u32[]{:S(2)}) %all-to-all-start.1) | async-done | bytes 1179680 | tf_op jit(solution)/shard_map/all_to_all | solution.py:224
  85.3 1.1 %combine.1 = bf16[16,8,1024]{2,1,0:T(8,128)(2,1)S(1)} custom-call(bf16[64,9,8,128]{3,2,1,0:T(8,128)(2,1)S(1)} %all-to-all-done.1.parts), custom_call_target="tpu_custom_call" | custom-call | tf_op jit(solution)/shard_map/combine/pallas_call | solution.py:180
  86.4 11.8 %all_to_all.16 = bf16[16,8,1024]{2,1,0:T(8,128)(2,1)S(1)} all-to-all(bf16[16,8,1024]{2,1,0:T(8,128)(2,1)S(1)} %combine.1), channel_id=1, replica_groups=mesh['y'=4,'z'=4,'core'=2,'head'=4] {'y','z'}, dimensions={0} | all-to-all | bytes 524288 | tf_op jit(solution)/shard_map/all_to_all | solution.py:224
  98.2 0.0 collective-permute-start.1
  98.2 0.0 collective-permute-done.2.w1
  98.2 0.0 collective-permute-done.3.w2
  98.2 0.0 collective-permute-done.4.w3
  98.2 1.5 %collective-permute-done.1 = bf16[16,8,1024]{2,1,0:T(8,128)(2,1)S(1)} collective-permute-done((bf16[16,8,1024]{2,1,0:T(8,128)(2,1)S(1)}, bf16[16,8,1024]{2,1,0:T(8,128)(2,1)S(1)}, u32[]{:S(2)}, u32[]{:S(2)}) %collective-permute-start.1) | collective-permute-done | bytes 262176 | tf_op jit(solution)/shard_map/ppermute | solution.py:220
  99.8 1.1 %mix.1 = bf16[64,256]{1,0:T(8,128)(2,1)} custom-call(s32[1]{0:T(128)} %bitcast.core, bf16[4,4,8,1024]{3,2,1,0:T(8,128)(2,1)S(1)} %bitcast.5, bf16[4,4,8,1024]{3,2,1,0:T(8,128)(2,1)S(1)} %bitcast.6, bf16[1024,256]{1,0:T(8,128)(2,1)S(1)} %copy-done.1, bf16[1024,256]{1,0:T(8,128)(2,1)S(1)} %collective-permute-done.2.w1, ...), custom_call_target="tpu_custom_call" | custom-call | tf_op jit(solution)/shard_map/mix/pallas_call | solution.py:209
Async XLA Ops:
  0.0 11.7 %copy-start.2 = (bf16[8,1024]{1,0:T(8,128)(2,1)S(1)}, bf16[8,1024]{1,0:T(8,128)(2,1)}, u32[]{:S(2)}) copy-start(bf16[8,1024]{1,0:T(8,128)(2,1)} %param.8) | copy-start | bytes 49156
  11.6 43.5 %copy-start.1 = (bf16[1024,256]{1,0:T(8,128)(2,1)S(1)}, bf16[1024,256]{1,0:T(8,128)(2,1)}, u32[]{:S(2)}) copy-start(bf16[1024,256]{1,0:T(8,128)(2,1)} %w0.1) | copy-start | bytes 1572868
  11.7 31.2 %collective-permute-start = (bf16[4,2,512,128]{3,2,1,0:T(8,128)(2,1)}, bf16[4,2,512,128]{3,2,1,0:T(8,128)(2,1)S(1)}, u32[]{:S(2)}, u32[]{:S(2)}) collective-permute-start(bf16[4,2,512,128]{3,2,1,0:T(8,128)(2,1)} %project.1.kv1), channel_id=1, source_target_pairs={{0,4},{4,0},{1,5},{5,1},{2,6},{6,2},{3,7},{7,3},{8,12},{12,8},{9,1... | collective-permute-start | bytes 3145736 | tf_op jit(solution)/shard_map/ppermute | solution.py:220
  42.8 1.2 %copy-start = (bf16[4,2,512,128]{3,2,1,0:T(8,128)(2,1)S(1)}, bf16[4,2,512,128]{3,2,1,0:T(8,128)(2,1)}, u32[]{:S(2)}) copy-start(bf16[4,2,512,128]{3,2,1,0:T(8,128)(2,1)} %project.1.kv1) | copy-start | bytes 3145732
  50.4 34.9 %all-to-all-start.1 = ((bf16[64,9,8,128]{3,2,1,0:T(8,128)(2,1)}), bf16[64,9,8,128]{3,2,1,0:T(8,128)(2,1)S(1)}, u32[]{:S(2)}, u32[]{:S(2)}) async-start(bf16[64,9,8,128]{3,2,1,0:T(8,128)(2,1)} %attend.1), calls=%async_computation.1 | async-start | bytes 2359296 | tf_op jit(solution)/shard_map/all_to_all | solution.py:224
  55.1 43.1 %collective-permute-start.2 = (bf16[1024,256]{1,0:T(8,128)(2,1)S(1)}, bf16[1024,256]{1,0:T(8,128)(2,1)S(1)}, u32[]{:S(2)}, u32[]{:S(2)}) collective-permute-start(bf16[1024,256]{1,0:T(8,128)(2,1)S(1)} %copy-done.1), channel_id=1, source_target_pairs={{1,0},{2,1},{3,2},{0,3},{5,4},{6,5},{7,6},{4,7},{9,8},{10,9},{11,1... | collective-permute-start | bytes 1572872 | tf_op jit(solution)/shard_map/ppermute | solution.py:228
  57.9 40.4 %collective-permute-start.3 = (bf16[1024,256]{1,0:T(8,128)(2,1)S(1)}, bf16[1024,256]{1,0:T(8,128)(2,1)S(1)}, u32[]{:S(2)}, u32[]{:S(2)}) collective-permute-start(bf16[1024,256]{1,0:T(8,128)(2,1)S(1)} %copy-done.1), channel_id=1, source_target_pairs={{2,0},{3,1},{0,2},{1,3},{6,4},{7,5},{4,6},{5,7},{10,8},{11,9},{8,1... | collective-permute-start | bytes 1572872 | tf_op jit(solution)/shard_map/ppermute | solution.py:228
  58.7 39.5 %collective-permute-start.4 = (bf16[1024,256]{1,0:T(8,128)(2,1)S(1)}, bf16[1024,256]{1,0:T(8,128)(2,1)S(1)}, u32[]{:S(2)}, u32[]{:S(2)}) collective-permute-start(bf16[1024,256]{1,0:T(8,128)(2,1)S(1)} %copy-done.1), channel_id=1, source_target_pairs={{3,0},{0,1},{1,2},{2,3},{7,4},{4,5},{5,6},{6,7},{11,8},{8,9},{9,10... | collective-permute-start | bytes 1572872 | tf_op jit(solution)/shard_map/ppermute | solution.py:228
  98.2 1.5 %collective-permute-start.1 = (bf16[16,8,1024]{2,1,0:T(8,128)(2,1)S(1)}, bf16[16,8,1024]{2,1,0:T(8,128)(2,1)S(1)}, u32[]{:S(2)}, u32[]{:S(2)}) collective-permute-start(bf16[16,8,1024]{2,1,0:T(8,128)(2,1)S(1)} %all_to_all.16), channel_id=1, source_target_pairs={{0,4},{4,0},{1,5},{5,1},{2,6},{6,2},{3,7},{7,3},{8,12},{12,8},{9,1... | collective-permute-start | bytes 786440 | tf_op jit(solution)/shard_map/ppermute | solution.py:220

commit v3 on v2

v3 whole, which is shorter than its diff:
```python
import math

import jax
import jax.numpy as jnp
from jax import lax
from jax.experimental import pallas as pl
from jax.experimental.pallas import tpu as pltpu
from jax.sharding import Mesh, PartitionSpec as P


HD = 128
GROUPS = 4
HEADS = 8
RPD = 8
PEERS = 16
ROWS = PEERS * RPD
STACK = 2
BLK = HEADS + 1
EXP2_SCALE = HD ** -0.5 * math.log2(math.e)
VMEM = pl.BlockSpec(memory_space=pltpu.VMEM)
HBM = pl.BlockSpec(memory_space=pltpu.HBM)
SMEM = pl.BlockSpec(memory_space=pltpu.SMEM)
YZ = ("y", "z")
YZX = ("y", "z", "head")
CHUNKS = (768,) * 10
AHEAD = 3


def limit(mib):
    return pltpu.CompilerParams(vmem_limit_bytes=mib * 1024 * 1024)


def project_kernel(x, wk, wv, out, twin, xb, wkb, wvb, acc, sems):
    offsets = [sum(CHUNKS[:i]) for i in range(len(CHUNKS))]
    copies = []
    for i, (at, size) in enumerate(zip(offsets, CHUNKS)):
        part = pl.ds(at, size)
        copies.append(
            [
                pltpu.make_async_copy(x.at[:, part], xb.at[:, part], sems.at[0, i]),
                pltpu.make_async_copy(wk.at[part, :], wkb.at[part, :], sems.at[1, i]),
                pltpu.make_async_copy(wv.at[part, :], wvb.at[part, :], sems.at[2, i]),
            ]
        )
    for i in range(AHEAD):
        for copy in copies[i]:
            copy.start()
    last = len(CHUNKS) - 1
    for i, (at, size) in enumerate(zip(offsets, CHUNKS)):
        for copy in copies[i]:
            copy.wait()
        if i + AHEAD <= last:
            for copy in copies[i + AHEAD]:
                copy.start()
        for j, w in enumerate((wkb, wvb)):
            part = jnp.dot(
                xb[:, at : at + size], w[at : at + size, :], preferred_element_type=jnp.float32
            )
            if i > 0:
                part = acc[j] + part
            if i < last:
                acc[j] = part
            else:
                for g in range(GROUPS):
                    mine = part[:, g * HD : (g + 1) * HD].astype(jnp.bfloat16)
                    out[g, j] = mine
                    twin[g, j] = mine


def project(vision, w_key, w_value):
    rows, width = vision.shape
    cols = w_key.shape[1]
    return pl.pallas_call(
        project_kernel,
        in_specs=[HBM] * 3,
        out_specs=[VMEM] * 2,
        out_shape=[
            pltpu.VMEM((GROUPS, 2, rows, HD), jnp.bfloat16),
            jax.ShapeDtypeStruct((GROUPS, 2, rows, HD), jnp.bfloat16),
        ],
        scratch_shapes=[
            pltpu.VMEM((rows, width), jnp.bfloat16),
            pltpu.VMEM((width, cols), jnp.bfloat16),
            pltpu.VMEM((width, cols), jnp.bfloat16),
            pltpu.VMEM((2, rows, cols), jnp.float32),
            pltpu.SemaphoreType.DMA((3, len(CHUNKS))),
        ],
        compiler_params=limit(56),
        name="project",
    )(vision, w_key, w_value)


def stats_tile(stats):
    count = stats.shape[0]
    mine = stats.reshape(count, 1, HD)
    high = mine.astype(jnp.bfloat16).astype(jnp.float32)
    rest = mine - high
    mid = rest.astype(jnp.bfloat16).astype(jnp.float32)
    low = rest - mid
    place = lax.broadcasted_iota(jnp.int32, (count, RPD, HD), 1)
    tile = jnp.where(
        place == 0, high, jnp.where(place == 1, mid, jnp.where(place == 2, low, 0.0))
    )
    return tile.astype(jnp.bfloat16)


def attend_kernel(group, q, kv1, kv2, out):
    tokens = kv1.shape[2]
    row = lax.broadcasted_iota(jnp.int32, (ROWS, HD), 0)
    lane = lax.broadcasted_iota(jnp.int32, (ROWS, HD), 1)
    contract = (((1,), (1,)), ((), ()))
    ones = jnp.ones((tokens, HD), jnp.bfloat16)
    g = group[0]
    k1, k2 = kv1[g, 0], kv2[g, 0]
    v1 = jnp.concatenate([kv1[g, 1], ones], axis=1)
    v2 = jnp.concatenate([kv2[g, 1], ones], axis=1)
    stats = jnp.zeros((ROWS, HD), jnp.float32)
    for first in range(0, HEADS, STACK):
        qs = [
            q[:, g, :, h * HD : (h + 1) * HD].reshape(ROWS, HD)
            for h in range(first, first + STACK)
        ]
        qs = jnp.concatenate(qs, axis=0)
        s1 = lax.dot_general(qs, k1, contract, preferred_element_type=jnp.float32)
        s2 = lax.dot_general(qs, k2, contract, preferred_element_type=jnp.float32)
        top = jnp.max(jnp.maximum(s1, s2), axis=1, keepdims=True)
        p1 = jnp.exp2((s1 - top) * EXP2_SCALE).astype(jnp.bfloat16)
        p2 = jnp.exp2((s2 - top) * EXP2_SCALE).astype(jnp.bfloat16)
        acc = jnp.dot(p1, v1, preferred_element_type=jnp.float32) + jnp.dot(
            p2, v2, preferred_element_type=jnp.float32
        )
        for k in range(STACK):
            h = first + k
            mine = acc[k * ROWS : (k + 1) * ROWS]
            out[:, h] = mine[:, :HD].reshape(PEERS, RPD, HD).astype(jnp.bfloat16)
            pair = h * RPD + row % RPD
            stats = jnp.where(lane == pair, top[k * ROWS : (k + 1) * ROWS], stats)
            stats = jnp.where(lane == HD // 2 + pair, mine[:, HD:], stats)
    out[:, HEADS] = stats_tile(jnp.sum(stats.reshape(PEERS, RPD, HD), axis=1))


def attend(group, q, kv1, kv2):
    return pl.pallas_call(
        attend_kernel,
        in_specs=[SMEM] + [VMEM] * 3,
        out_specs=VMEM,
        out_shape=jax.ShapeDtypeStruct((PEERS, BLK, RPD, HD), jnp.bfloat16),
        compiler_params=limit(32),
        name="attend",
    )(group, q, kv1, kv2)


def read_stats(part):
    stats = jnp.sum(part[:, HEADS].astype(jnp.float32), axis=1)
    return stats[:, : HD // 2], stats[:, HD // 2 :]


def merge_kernel(*refs):
    sources, out = refs[:-1], refs[-1]
    stats = [read_stats(part) for part in sources]
    top = stats[0][0]
    for maxima, _ in stats[1:]:
        top = jnp.maximum(top, maxima)
    total = jnp.zeros_like(top)
    weights = []
    for maxima, sums in stats:
        factor = jnp.exp2((maxima - top) * EXP2_SCALE)
        total = total + factor * sums
        weights.append(factor.T)
    for p in range(PEERS):
        acc = jnp.zeros((HEADS * RPD, HD), jnp.float32)
        for part, weight in zip(sources, weights):
            value = part[p, :HEADS].astype(jnp.float32).reshape(HEADS * RPD, HD)
            acc = acc + value * weight[:, p : p + 1]
        out[p, :HEADS] = acc.reshape(HEADS, RPD, HD).astype(jnp.bfloat16)
    out[:, HEADS] = stats_tile(jnp.concatenate([top, total], axis=1))


def merge(parts):
    return pl.pallas_call(
        merge_kernel,
        in_specs=[VMEM] * len(parts),
        out_specs=VMEM,
        out_shape=jax.ShapeDtypeStruct((PEERS, BLK, RPD, HD), jnp.bfloat16),
        compiler_params=limit(8),
        name="merge",
    )(*parts)


def combine_kernel(parts, out):
    maxima, sums = read_stats(parts)
    top = jnp.max(maxima, axis=0, keepdims=True)
    factor = jnp.exp2((maxima - top) * EXP2_SCALE)
    denom = jnp.sum(factor * sums, axis=0, keepdims=True)
    weight = (factor / denom).T
    total = jnp.zeros((HEADS * RPD, HD), jnp.float32)
    for s in range(PEERS):
        block = parts[s, :HEADS].astype(jnp.float32).reshape(HEADS * RPD, HD)
        total = total + block * weight[:, s : s + 1]
    total = total.reshape(HEADS, RPD, HD)
    row = jnp.concatenate([total[h] for h in range(HEADS)], axis=1).astype(jnp.bfloat16)
    for s in range(PEERS):
        out[s] = row


def combine(parts):
    return pl.pallas_call(
        combine_kernel,
        in_specs=[VMEM],
        out_specs=VMEM,
        out_shape=jax.ShapeDtypeStruct((PEERS, RPD, HEADS * HD), jnp.bfloat16),
        compiler_params=limit(8),
        name="combine",
    )(parts)


def mix_kernel(core, rows, own, other, out):
    cols = own.shape[1]
    shape = (GROUPS, 1, ROWS // GROUPS, cols)
    flat = rows[...].reshape(ROWS, -1)
    for w, place in ((own, core[0]), (other, 1 - core[0])):
        part = jnp.dot(flat, w[...], preferred_element_type=jnp.float32)
        out[:, pl.ds(place, 1)] = part.reshape(shape).astype(jnp.bfloat16)


def mix(core, rows, own, other):
    return pl.pallas_call(
        mix_kernel,
        in_specs=[SMEM] + [VMEM] * 3,
        out_specs=VMEM,
        out_shape=jax.ShapeDtypeStruct((GROUPS, 2, ROWS // GROUPS, own.shape[1]), jnp.bfloat16),
        compiler_params=limit(8),
        name="mix",
    )(core, rows, own, other)


def swap_cores(x):
    return lax.ppermute(x, "core", [(0, 1), (1, 0)])


def exchange(x, axes):
    return lax.all_to_all(x, axes, split_axis=0, concat_axis=0, tiled=True)


def send_block(x, way):
    pairs = [
        (c * GROUPS + i, c * GROUPS + (i + (-way if c == 0 else way)) % GROUPS)
        for c in range(2)
        for i in range(GROUPS)
    ]
    return lax.ppermute(x, ("core", "head"), pairs)


def index_of(axis):
    return lax.axis_index(axis).astype(jnp.int32).reshape(1)


def shards(vision, w_key, w_value, queries, w_out):
    copies = jnp.broadcast_to(queries[None], (PEERS * GROUPS,) + queries.shape)
    rows = exchange(copies, YZX).reshape(PEERS, GROUPS, RPD, -1)
    kv1, twin = project(vision, w_key, w_value)
    kv2 = swap_cores(twin)
    head, core = index_of("head"), index_of("core")
    way = 2 * core - 1

    def attend_for(ahead):
        return attend((head + ahead + GROUPS) % GROUPS, rows, kv1, kv2)

    far = send_block(attend_for(2 * way), 1)
    back = send_block(attend_for(-way), -1)
    near = merge([attend_for(way), far])
    near = send_block(near, 1)
    part = merge([attend_for(0 * way), back, near])
    w_other = swap_cores(w_out)
    attended = exchange(combine(exchange(part, YZ)), YZ)
    partial = mix(core, attended, w_out, w_other)
    shape = partial.shape[2:]
    shares = exchange(partial.reshape((-1,) + shape), ("head", "core"))
    shares = shares.reshape(GROUPS, 2, GROUPS, RPD, -1).astype(jnp.float32)
    total = jnp.sum(shares, axis=0).transpose(1, 0, 2, 3)
    return total.reshape(2 * GROUPS * RPD, -1).astype(jnp.bfloat16)


def solution(mesh):
    fine = Mesh(mesh.devices.reshape(4, 4, 2, 4), ("y", "z", "core", "head"))
    seq = ("y", "z", "core")
    placed = (P(seq + ("head",), None), P(), P(), P(seq, "head"), P("head", seq))
    return jax.shard_map(
        shards, mesh=fine, in_specs=placed, out_specs=P("head", seq), check_vma=False
    )
```

time: 102 us -> 101 us (level)
  blocking collectives: 42.7 us -> 20.9 us
  waiting for transfers between devices: 27.3 us -> 36.9 us
  starting transfers between devices: 9.2 us -> 17.8 us
  Pallas kernels: 20.2 us -> 22.4 us
    all_to_all x2, blocking collectives: 42.7 us -> 20.9 us  [exchange(): return lax.all_to_all(x, axes, split_axis=0, concat_axis=0, tiled=True)]
    all_to_all x1 -> x2, starting transfers between devices: 4.66 us -> 15.2 us  [exchange(): return lax.all_to_all(x, axes, split_axis=0, concat_axis=0, tiled=True)]
    ppermute x3, waiting for transfers between devices: 0.01 us -> 8.89 us  [send_block(): return lax.ppermute(x, ('core', 'head'), pairs)]
    all_to_all x1 -> x2, waiting for transfers between devices: 25.8 us -> 28 us  [exchange(): return lax.all_to_all(x, axes, split_axis=0, concat_axis=0, tiled=True)]
    ppermute x3, starting transfers between devices: 4.46 us -> 2.25 us  [send_block(): return lax.ppermute(x, ('core', 'head'), pairs)]
    pallas_call x3 -> x8, Pallas kernels: 19.1 us -> 21.3 us  [the longest x1 11.6 us: project(): pl.pallas_call(project_kernel, in_specs=[HBM] * 3, out_specs=[VMEM] * 2,...]
    ppermute x2, waiting for transfers between devices: 1.52 us -> 0.01 us  [swap_cores(): return lax.ppermute(x, 'core', [(0, 1), (1, 0)])]
    unnamed x6 -> x2, local copies, waits for them, and re-layouts: 1.24 us -> 0.01 us
  transfers between devices with their start and end apart: 6 -> 7, of which waited for: 2 -> 4; matrix products, arithmetic and copies ran while one was open for 0% -> 1% of each run, Pallas kernels for 1% -> 8%
where the time goes in v3:
time: 101 us; the launch traced here: 100 us
  waiting for transfers between devices  36.9 us (37%)
  Pallas kernels  22.4 us (22%)
  blocking collectives  20.9 us (21%)
  starting transfers between devices  17.8 us (18%)
  local copies, waits for them, and re-layouts  1.78 us (2%)
    all_to_all x2, waiting for transfers between devices, exchange(): return lax.all_to_all(x, axes, split_axis=0, concat_axis=0, tiled=True)  28 us
    all_to_all x2, blocking collectives, exchange(): return lax.all_to_all(x, axes, split_axis=0, concat_axis=0, tiled=True)  20.9 us
    all_to_all x2, starting transfers between devices, exchange(): return lax.all_to_all(x, axes, split_axis=0, concat_axis=0, tiled=True)  15.2 us
    pallas_call x1, Pallas kernels, project(): pl.pallas_call(project_kernel, in_specs=[HBM] * 3, out_specs=[VMEM] * 2,...  11.6 us
    ppermute x3, waiting for transfers between devices, send_block(): return lax.ppermute(x, ('core', 'head'), pairs)  8.89 us
    pallas_call x4, Pallas kernels, attend(): pl.pallas_call(attend_kernel, in_specs=[SMEM] + [VMEM] * 3, out_specs=VME...  6.96 us
    ppermute x3, starting transfers between devices, send_block(): return lax.ppermute(x, ('core', 'head'), pairs)  2.25 us
  transfers between devices with their start and end apart: 7, of which 4 were waited for; matrix products, arithmetic and copies ran while one was open for 1% of the time, Pallas kernels for 8%

profile of v3, /device:TPU:0, one launch (start us, length us, event | category | flops | bytes accessed | tf_op | source)
XLA Modules:
  0.0 100.0 jit_solution(15578885719754535224)
XLA Ops:
  0.0 0.0 copy-start
  0.0 11.6 %project.1 = (bf16[4,2,512,128]{3,2,1,0:T(8,128)(2,1)S(1)}, bf16[4,2,512,128]{3,2,1,0:T(8,128)(2,1)}) custom-call(bf16[512,7680]{1,0:T(8,128)(2,1)} %x.1, bf16[7680,512]{1,0:T(8,128)(2,1)} %wk.1, bf16[7680,512]{1,0:T(8,128)(2,1)} %wv.1), custom_call_target="tpu_custom_call" | custom-call | tf_op jit(solution)/shard_map/project/pallas_call | solution.py:73
  11.6 0.1 collective-permute-start
  11.7 0.0 copy-done
  11.7 1.2 %broadcast_in_dim.2 = bf16[64,8,1024]{2,1,0:T(8,128)(2,1)} broadcast(bf16[8,1024]{1,0:T(8,128)(2,1)S(1)} %copy-done), dimensions={1,2} | broadcast | bytes 1064960 | tf_op jit(solution)/shard_map/broadcast_in_dim | solution.py:259
  12.9 11.5 %all-to-all-start = ((bf16[64,8,1024]{2,1,0:T(8,128)(2,1)}), bf16[64,8,1024]{2,1,0:T(8,128)(2,1)S(1)}, u32[]{:S(2)}, u32[]{:S(2)}) async-start(bf16[64,8,1024]{2,1,0:T(8,128)(2,1)} %broadcast_in_dim.2), calls=%async_computation | async-start | bytes 2097152 | tf_op jit(solution)/shard_map/all_to_all | solution.py:242
  24.5 19.6 %all-to-all-done = bf16[64,8,1024]{2,1,0:T(8,128)(2,1)S(1)} async-done(((bf16[64,8,1024]{2,1,0:T(8,128)(2,1)}), bf16[64,8,1024]{2,1,0:T(8,128)(2,1)S(1)}, u32[]{:S(2)}, u32[]{:S(2)}) %all-to-all-start) | async-done | bytes 1048608 | tf_op jit(solution)/shard_map/all_to_all | solution.py:242
  44.0 0.0 collective-permute-done.kv2
  44.0 1.7 %attend.7 = bf16[16,9,8,128]{3,2,1,0:T(8,128)(2,1)S(1)} custom-call(s32[1]{0:T(128)S(6)} %select_n.22.group, bf16[16,4,8,1024]{3,2,1,0:T(8,128)(2,1)S(1)} %bitcast.7, bf16[4,2,512,128]{3,2,1,0:T(8,128)(2,1)S(1)} %get-tuple-element.7.kv1, bf16[4,2,512,128]{3,2,1,0:T(8,128)(2,1)S(1)} %collective-permute-done.kv2), custom_call_target="tpu_custom_call" | custom-call | tf_op jit(solution)/shard_map/attend/pallas_call | solution.py:143
  45.8 0.9 collective-permute-start.2
  46.7 1.7 %attend.5 = bf16[16,9,8,128]{3,2,1,0:T(8,128)(2,1)S(1)} custom-call(s32[1]{0:T(128)S(6)} %select_n.20.group, bf16[16,4,8,1024]{3,2,1,0:T(8,128)(2,1)S(1)} %bitcast.8, bf16[4,2,512,128]{3,2,1,0:T(8,128)(2,1)S(1)} %get-tuple-element.7.kv1, bf16[4,2,512,128]{3,2,1,0:T(8,128)(2,1)S(1)} %collective-permute-done.kv2), custom_call_target="tpu_custom_call" | custom-call | tf_op jit(solution)/shard_map/attend/pallas_call | solution.py:143
  48.4 1.3 %collective-permute-start.1 = (bf16[16,9,8,128]{3,2,1,0:T(8,128)(2,1)S(1)}, bf16[16,9,8,128]{3,2,1,0:T(8,128)(2,1)S(1)}, u32[]{:S(2)}, u32[]{:S(2)}) collective-permute-start(bf16[16,9,8,128]{3,2,1,0:T(8,128)(2,1)S(1)} %attend.5), channel_id=1, source_target_pairs={{0,1},{1,2},{2,3},{3,0},{4,7},{5,4},{6,5},{7,6},{8,9},{9,10},{10,1... | collective-permute-start | bytes 884744 | tf_op jit(solution)/shard_map/ppermute | solution.py:251
  49.7 1.7 %attend.6.refs_0_ = bf16[16,9,8,128]{3,2,1,0:T(8,128)(2,1)S(1)} custom-call(s32[1]{0:T(128)S(6)} %select_n.21.group, bf16[16,4,8,1024]{3,2,1,0:T(8,128)(2,1)S(1)} %bitcast.9, bf16[4,2,512,128]{3,2,1,0:T(8,128)(2,1)S(1)} %get-tuple-element.7.kv1, bf16[4,2,512,128]{3,2,1,0:T(8,128)(2,1)S(1)} %collective-permute-done.kv2), custom_call_target="tpu_custom_call" | custom-call | tf_op jit(solution)/shard_map/attend/pallas_call | solution.py:143
  51.4 4.2 %collective-permute-done.2.refs_1_ = bf16[16,9,8,128]{3,2,1,0:T(8,128)(2,1)S(1)} collective-permute-done((bf16[16,9,8,128]{3,2,1,0:T(8,128)(2,1)S(1)}, bf16[16,9,8,128]{3,2,1,0:T(8,128)(2,1)S(1)}, u32[]{:S(2)}, u32[]{:S(2)}) %collective-permute-start.2) | collective-permute-done | bytes 294944 | tf_op jit(solution)/shard_map/ppermute | solution.py:251
  55.7 0.5 merge.2
  56.2 0.1 collective-permute-start.3
  56.3 0.3 collective-permute-start.4
  56.6 1.7 %attend.4.refs_0_ = bf16[16,9,8,128]{3,2,1,0:T(8,128)(2,1)S(1)} custom-call(s32[1]{0:T(128)S(6)} %select_n.19.group, bf16[16,4,8,1024]{3,2,1,0:T(8,128)(2,1)S(1)} %bitcast.10, bf16[4,2,512,128]{3,2,1,0:T(8,128)(2,1)S(1)} %get-tuple-element.7.kv1, bf16[4,2,512,128]{3,2,1,0:T(8,128)(2,1)S(1)} %collective-permute-done.kv2), custom_call_target="tpu_custom_call" | custom-call | tf_op jit(solution)/shard_map/attend/pallas_call | solution.py:143
  58.3 0.0 collective-permute-done.1.refs_1_
  58.3 4.7 %collective-permute-done.3.refs_2_ = bf16[16,9,8,128]{3,2,1,0:T(8,128)(2,1)S(1)} collective-permute-done((bf16[16,9,8,128]{3,2,1,0:T(8,128)(2,1)S(1)}, bf16[16,9,8,128]{3,2,1,0:T(8,128)(2,1)S(1)}, u32[]{:S(2)}, u32[]{:S(2)}) %collective-permute-start.3) | collective-permute-done | bytes 294944 | tf_op jit(solution)/shard_map/ppermute | solution.py:251
  63.0 0.7 merge.3
  63.7 11.2 %all_to_all.20.parts = bf16[16,9,8,128]{3,2,1,0:T(8,128)(2,1)S(1)} all-to-all(bf16[16,9,8,128]{3,2,1,0:T(8,128)(2,1)S(1)} %merge.3), channel_id=1, replica_groups=mesh['y'=4,'z'=4,'core'=2,'head'=4] {'y','z'}, dimensions={0} | all-to-all | bytes 589824 | tf_op jit(solution)/shard_map/all_to_all | solution.py:242
  74.9 1.1 %combine.1 = bf16[16,8,1024]{2,1,0:T(8,128)(2,1)} custom-call(bf16[16,9,8,128]{3,2,1,0:T(8,128)(2,1)S(1)} %all_to_all.20.parts), custom_call_target="tpu_custom_call" | custom-call | tf_op jit(solution)/shard_map/combine/pallas_call | solution.py:207
  76.1 3.7 %all-to-all-start.2 = ((bf16[16,8,1024]{2,1,0:T(8,128)(2,1)}), bf16[16,8,1024]{2,1,0:T(8,128)(2,1)S(1)}, u32[]{:S(2)}, u32[]{:S(2)}) async-start(bf16[16,8,1024]{2,1,0:T(8,128)(2,1)} %combine.1), calls=%async_computation.2 | async-start | bytes 524288 | tf_op jit(solution)/shard_map/all_to_all | solution.py:242
  79.7 0.0 collective-permute-done.4.other
  79.7 8.5 %all-to-all-done.2.rows = bf16[16,8,1024]{2,1,0:T(8,128)(2,1)S(1)} async-done(((bf16[16,8,1024]{2,1,0:T(8,128)(2,1)}), bf16[16,8,1024]{2,1,0:T(8,128)(2,1)S(1)}, u32[]{:S(2)}, u32[]{:S(2)}) %all-to-all-start.2) | async-done | bytes 262176 | tf_op jit(solution)/shard_map/all_to_all | solution.py:242
  88.2 1.5 %mix.1 = bf16[4,2,32,256]{3,2,1,0:T(8,128)(2,1)S(1)} custom-call(s32[1]{0:T(128)} %bitcast.core, bf16[16,8,1024]{2,1,0:T(8,128)(2,1)S(1)} %all-to-all-done.2.rows, bf16[1024,256]{1,0:T(8,128)(2,1)} %own.1, bf16[1024,256]{1,0:T(8,128)(2,1)} %collective-permute-done.4.other), custom_call_target="tpu_custom_call" | custom-call | tf_op jit(solution)/shard_map/mix/pallas_call | solution.py:227
  89.7 9.6 %all_to_all.21 = bf16[8,32,256]{2,1,0:T(8,128)(2,1)S(1)} all-to-all(bf16[8,32,256]{2,1,0:T(8,128)(2,1)S(1)} %bitcast.11), channel_id=1, replica_groups=mesh['y'=4,'z'=4,'core'=2,'head'=4] {'head','core'}, dimensions={0} | all-to-all | bytes 262144 | tf_op jit(solution)/shard_map/all_to_all | solution.py:242
  99.4 0.6 copy.6
  (1 shorter events, 0.0 us)
Async XLA Ops:
  0.0 11.7 %copy-start = (bf16[8,1024]{1,0:T(8,128)(2,1)S(1)}, bf16[8,1024]{1,0:T(8,128)(2,1)}, u32[]{:S(2)}) copy-start(bf16[8,1024]{1,0:T(8,128)(2,1)} %param.8) | copy-start | bytes 49156
  11.6 32.4 %collective-permute-start = (bf16[4,2,512,128]{3,2,1,0:T(8,128)(2,1)}, bf16[4,2,512,128]{3,2,1,0:T(8,128)(2,1)S(1)}, u32[]{:S(2)}, u32[]{:S(2)}) collective-permute-start(bf16[4,2,512,128]{3,2,1,0:T(8,128)(2,1)} %get-tuple-element.8), channel_id=1, source_target_pairs={{0,4},{4,0},{1,5},{5,1},{2,6},{6,2},{3,7},{7,3},{8,12},{12,8},{9,1... | collective-permute-start | bytes 3145736 | tf_op jit(solution)/shard_map/ppermute | solution.py:238
  12.9 31.1 %all-to-all-start = ((bf16[64,8,1024]{2,1,0:T(8,128)(2,1)}), bf16[64,8,1024]{2,1,0:T(8,128)(2,1)S(1)}, u32[]{:S(2)}, u32[]{:S(2)}) async-start(bf16[64,8,1024]{2,1,0:T(8,128)(2,1)} %broadcast_in_dim.2), calls=%async_computation | async-start | bytes 2097152 | tf_op jit(solution)/shard_map/all_to_all | solution.py:242
  45.8 9.9 %collective-permute-start.2 = (bf16[16,9,8,128]{3,2,1,0:T(8,128)(2,1)S(1)}, bf16[16,9,8,128]{3,2,1,0:T(8,128)(2,1)S(1)}, u32[]{:S(2)}, u32[]{:S(2)}) collective-permute-start(bf16[16,9,8,128]{3,2,1,0:T(8,128)(2,1)S(1)} %attend.7), channel_id=1, source_target_pairs={{0,3},{1,0},{2,1},{3,2},{4,5},{5,6},{6,7},{7,4},{8,11},{9,8},{10,9... | collective-permute-start | bytes 884744 | tf_op jit(solution)/shard_map/ppermute | solution.py:251
  48.4 9.9 %collective-permute-start.1 = (bf16[16,9,8,128]{3,2,1,0:T(8,128)(2,1)S(1)}, bf16[16,9,8,128]{3,2,1,0:T(8,128)(2,1)S(1)}, u32[]{:S(2)}, u32[]{:S(2)}) collective-permute-start(bf16[16,9,8,128]{3,2,1,0:T(8,128)(2,1)S(1)} %attend.5), channel_id=1, source_target_pairs={{0,1},{1,2},{2,3},{3,0},{4,7},{5,4},{6,5},{7,6},{8,9},{9,10},{10,1... | collective-permute-start | bytes 884744 | tf_op jit(solution)/shard_map/ppermute | solution.py:251
  56.2 6.8 %collective-permute-start.3 = (bf16[16,9,8,128]{3,2,1,0:T(8,128)(2,1)S(1)}, bf16[16,9,8,128]{3,2,1,0:T(8,128)(2,1)S(1)}, u32[]{:S(2)}, u32[]{:S(2)}) collective-permute-start(bf16[16,9,8,128]{3,2,1,0:T(8,128)(2,1)S(1)} %merge.2), channel_id=1, source_target_pairs={{0,3},{1,0},{2,1},{3,2},{4,5},{5,6},{6,7},{7,4},{8,11},{9,8},{10,9... | collective-permute-start | bytes 884744 | tf_op jit(solution)/shard_map/ppermute | solution.py:251
  56.3 23.5 %collective-permute-start.4 = (bf16[1024,256]{1,0:T(8,128)(2,1)}, bf16[1024,256]{1,0:T(8,128)(2,1)}, u32[]{:S(2)}, u32[]{:S(2)}) collective-permute-start(bf16[1024,256]{1,0:T(8,128)(2,1)} %own.1), channel_id=1, source_target_pairs={{0,4},{4,0},{1,5},{5,1},{2,6},{6,2},{3,7},{7,3},{8,12},{12,8},{9,1... | collective-permute-start | bytes 1572872 | tf_op jit(solution)/shard_map/ppermute | solution.py:238
  76.1 12.2 %all-to-all-start.2 = ((bf16[16,8,1024]{2,1,0:T(8,128)(2,1)}), bf16[16,8,1024]{2,1,0:T(8,128)(2,1)S(1)}, u32[]{:S(2)}, u32[]{:S(2)}) async-start(bf16[16,8,1024]{2,1,0:T(8,128)(2,1)} %combine.1), calls=%async_computation.2 | async-start | bytes 524288 | tf_op jit(solution)/shard_map/all_to_all | solution.py:242

commit v4 on v3

--- a/solution.py
+++ b/solution.py
@@ -21,16 +21,17 @@
 HBM = pl.BlockSpec(memory_space=pltpu.HBM)
 SMEM = pl.BlockSpec(memory_space=pltpu.SMEM)
 YZ = ("y", "z")
-YZX = ("y", "z", "head")
 CHUNKS = (768,) * 10
 AHEAD = 3
+AHEADS = (0, 0, 2, 1, -1)
 
 
 def limit(mib):
     return pltpu.CompilerParams(vmem_limit_bytes=mib * 1024 * 1024)
 
 
-def project_kernel(x, wk, wv, out, twin, xb, wkb, wvb, acc, sems):
+def project_kernel(head, way, x, wk, wv, *rest):
+    outs, (xb, wkb, wvb, acc, sems) = rest[: len(AHEADS)], rest[len(AHEADS) :]
     offsets = [sum(CHUNKS[:i]) for i in range(len(CHUNKS))]
     copies = []
     for i, (at, size) in enumerate(zip(offsets, CHUNKS)):
@@ -63,21 +64,22 @@
             else:
                 for g in range(GROUPS):
                     mine = part[:, g * HD : (g + 1) * HD].astype(jnp.bfloat16)
-                    out[g, j] = mine
-                    twin[g, j] = mine
-
-
-def project(vision, w_key, w_value):
+                    for ahead, out in zip(AHEADS, outs):
+
+                        @pl.when((head[0] + ahead * way[0] + GROUPS) % GROUPS == g)
+                        def _(out=out, mine=mine):
+                            out[j] = mine
+
+
+def project(head, way, vision, w_key, w_value):
     rows, width = vision.shape
     cols = w_key.shape[1]
     return pl.pallas_call(
         project_kernel,
-        in_specs=[HBM] * 3,
-        out_specs=[VMEM] * 2,
-        out_shape=[
-            pltpu.VMEM((GROUPS, 2, rows, HD), jnp.bfloat16),
-            jax.ShapeDtypeStruct((GROUPS, 2, rows, HD), jnp.bfloat16),
-        ],
+        in_specs=[SMEM] * 2 + [HBM] * 3,
+        out_specs=[VMEM] * len(AHEADS),
+        out_shape=[pltpu.VMEM((2, rows, HD), jnp.bfloat16)]
+        + [jax.ShapeDtypeStruct((2, rows, HD), jnp.bfloat16)] * GROUPS,
         scratch_shapes=[
             pltpu.VMEM((rows, width), jnp.bfloat16),
             pltpu.VMEM((width, cols), jnp.bfloat16),
@@ -87,7 +89,7 @@
         ],
         compiler_params=limit(56),
         name="project",
-    )(vision, w_key, w_value)
+    )(head, way, vision, w_key, w_value)
 
 
 def stats_tile(stats):
@@ -104,20 +106,19 @@
     return tile.astype(jnp.bfloat16)
 
 
-def attend_kernel(group, q, kv1, kv2, out):
-    tokens = kv1.shape[2]
+def attend_kernel(q, kv1, kv2, out):
+    tokens = kv1.shape[1]
     row = lax.broadcasted_iota(jnp.int32, (ROWS, HD), 0)
     lane = lax.broadcasted_iota(jnp.int32, (ROWS, HD), 1)
     contract = (((1,), (1,)), ((), ()))
     ones = jnp.ones((tokens, HD), jnp.bfloat16)
-    g = group[0]
-    k1, k2 = kv1[g, 0], kv2[g, 0]
-    v1 = jnp.concatenate([kv1[g, 1], ones], axis=1)
-    v2 = jnp.concatenate([kv2[g, 1], ones], axis=1)
+    k1, k2 = kv1[0], kv2[0]
+    v1 = jnp.concatenate([kv1[1], ones], axis=1)
+    v2 = jnp.concatenate([kv2[1], ones], axis=1)
     stats = jnp.zeros((ROWS, HD), jnp.float32)
     for first in range(0, HEADS, STACK):
         qs = [
-            q[:, g, :, h * HD : (h + 1) * HD].reshape(ROWS, HD)
+            q[:, :, h * HD : (h + 1) * HD].reshape(ROWS, HD)
             for h in range(first, first + STACK)
         ]
         qs = jnp.concatenate(qs, axis=0)
@@ -139,15 +140,15 @@
     out[:, HEADS] = stats_tile(jnp.sum(stats.reshape(PEERS, RPD, HD), axis=1))
 
 
-def attend(group, q, kv1, kv2):
+def attend(q, kv1, kv2):
     return pl.pallas_call(
         attend_kernel,
-        in_specs=[SMEM] + [VMEM] * 3,
+        in_specs=[VMEM] * 3,
         out_specs=VMEM,
         out_shape=jax.ShapeDtypeStruct((PEERS, BLK, RPD, HD), jnp.bfloat16),
-        compiler_params=limit(32),
+        compiler_params=limit(24),
         name="attend",
-    )(group, q, kv1, kv2)
+    )(q, kv1, kv2)
 
 
 def read_stats(part):
@@ -256,21 +257,18 @@
 
 
 def shards(vision, w_key, w_value, queries, w_out):
-    copies = jnp.broadcast_to(queries[None], (PEERS * GROUPS,) + queries.shape)
-    rows = exchange(copies, YZX).reshape(PEERS, GROUPS, RPD, -1)
-    kv1, twin = project(vision, w_key, w_value)
-    kv2 = swap_cores(twin)
+    copies = jnp.broadcast_to(queries[None], (PEERS,) + queries.shape)
+    rows = exchange(copies, YZ)
     head, core = index_of("head"), index_of("core")
-    way = 2 * core - 1
-
-    def attend_for(ahead):
-        return attend((head + ahead + GROUPS) % GROUPS, rows, kv1, kv2)
-
-    far = send_block(attend_for(2 * way), 1)
-    back = send_block(attend_for(-way), -1)
-    near = merge([attend_for(way), far])
+    own, twin, far, near, back = project(head, 2 * core - 1, vision, w_key, w_value)
+    far = send_block(far, 2)
     near = send_block(near, 1)
-    part = merge([attend_for(0 * way), back, near])
+    back = send_block(back, -1)
+    parts = [
+        attend(rows, kv, swap_cores(sent))
+        for kv, sent in ((own, twin), (near, near), (back, back), (far, far))
+    ]
+    part = merge(parts)
     w_other = swap_cores(w_out)
     attended = exchange(combine(exchange(part, YZ)), YZ)
     partial = mix(core, attended, w_out, w_other)

time: 101 us -> 91.5 us (0.906)
  waiting for transfers between devices: 36.9 us -> 27.7 us
    all_to_all x2, waiting for transfers between devices: 28 us -> 17.1 us  [exchange(): return lax.all_to_all(x, axes, split_axis=0, concat_axis=0, tiled=True)]
    all_to_all x2, starting transfers between devices: 15.2 us -> 11.7 us  [exchange(): return lax.all_to_all(x, axes, split_axis=0, concat_axis=0, tiled=True)]
    ppermute x3, starting transfers between devices: 2.25 us -> 5.24 us  [send_block(): return lax.ppermute(x, ('core', 'head'), pairs)]
    ppermute x3, waiting for transfers between devices: 8.89 us -> 10.6 us  [send_block(): return lax.ppermute(x, ('core', 'head'), pairs)]
    pallas_call x1, Pallas kernels: 1.51 us -> 0.31 us  [mix(): pl.pallas_call(mix_kernel, in_specs=[SMEM] + [VMEM] * 3, out_specs=VMEM,...]
  transfers between devices with their start and end apart: 7 -> 10, of which waited for: 4 -> 4; matrix products, arithmetic and copies ran while one was open for 1% -> 1% of each run, Pallas kernels for 8% -> 10%
where the time goes in v4:
time: 91.5 us; the launch traced here: 90.6 us
  waiting for transfers between devices  27.7 us (30%)
  Pallas kernels  21.7 us (24%)
  blocking collectives  21.7 us (24%)
  starting transfers between devices  17.9 us (20%)
  local copies, waits for them, and re-layouts  1.37 us (1%)
    all_to_all x2, blocking collectives, exchange(): return lax.all_to_all(x, axes, split_axis=0, concat_axis=0, tiled=True)  21.7 us
    all_to_all x2, waiting for transfers between devices, exchange(): return lax.all_to_all(x, axes, split_axis=0, concat_axis=0, tiled=True)  17.1 us
    pallas_call x1, Pallas kernels, project(): pl.pallas_call(project_kernel, in_specs=[SMEM] * 2 + [HBM] * 3, out_specs...  12.5 us
    all_to_all x2, starting transfers between devices, exchange(): return lax.all_to_all(x, axes, split_axis=0, concat_axis=0, tiled=True)  11.7 us
    ppermute x3, waiting for transfers between devices, send_block(): return lax.ppermute(x, ('core', 'head'), pairs)  10.6 us
    pallas_call x4, Pallas kernels, attend(): pl.pallas_call(attend_kernel, in_specs=[VMEM] * 3, out_specs=VMEM, out_sh...  6.97 us
    ppermute x3, starting transfers between devices, send_block(): return lax.ppermute(x, ('core', 'head'), pairs)  5.24 us
  transfers between devices with their start and end apart: 10, of which 4 were waited for; matrix products, arithmetic and copies ran while one was open for 1% of the time, Pallas kernels for 10%

profile of v4, /device:TPU:0, one launch (start us, length us, event | category | flops | bytes accessed | tf_op | source)
XLA Modules:
  0.0 90.6 jit_solution(400668462498666158)
XLA Ops:
  0.0 0.0 copy-start.1
  0.0 0.0 copy-start
  0.0 12.5 %project.1 = (bf16[2,512,128]{2,1,0:T(8,128)(2,1)S(1)}, bf16[2,512,128]{2,1,0:T(8,128)(2,1)}, bf16[2,512,128]{2,1,0:T(8,128)(2,1)}, bf16[2,512,128]{2,1,0:T(8,128)(2,1)}, bf16[2,512,128]{2,1,0:T(8,128)(2,1)}) custom-call(s32[1]{0:T(128)} %bitcast.1.head, s32[1]{0:T(128)S(6)} %sub.3.way, bf16[512,7680]{1,0:T(8,128)(2,1)} %x.1, bf16[7680,512]{1,0:T(8,128)(2,1)} %wk.1, ...), custom_call_target="tpu_custom_call" | custom-call | tf_op jit(solution)/shard_map/project/pallas_call | solution.py:77
  12.5 2.9 %collective-permute-start.1 = (bf16[2,512,128]{2,1,0:T(8,128)(2,1)}, bf16[2,512,128]{2,1,0:T(8,128)(2,1)S(1)}, u32[]{:S(2)}, u32[]{:S(2)}) collective-permute-start(bf16[2,512,128]{2,1,0:T(8,128)(2,1)} %get-tuple-element.12), channel_id=1, source_target_pairs={{0,3},{1,0},{2,1},{3,2},{4,5},{5,6},{6,7},{7,4},{8,11},{9,8},{10,9... | collective-permute-start | bytes 786440 | tf_op jit(solution)/shard_map/ppermute | solution.py:252
  15.4 0.0 collective-permute-start.3
  15.4 2.3 %collective-permute-start.5 = (bf16[2,512,128]{2,1,0:T(8,128)(2,1)}, bf16[2,512,128]{2,1,0:T(8,128)(2,1)S(1)}, u32[]{:S(2)}, u32[]{:S(2)}) collective-permute-start(bf16[2,512,128]{2,1,0:T(8,128)(2,1)} %get-tuple-element.14), channel_id=1, source_target_pairs={{0,2},{1,3},{2,0},{3,1},{4,6},{5,7},{6,4},{7,5},{8,10},{9,11},{10,... | collective-permute-start | bytes 786440 | tf_op jit(solution)/shard_map/ppermute | solution.py:252
  17.7 0.0 collective-permute-start
  17.7 9.3 %collective-permute-done.1.kv1 = bf16[2,512,128]{2,1,0:T(8,128)(2,1)S(1)} collective-permute-done((bf16[2,512,128]{2,1,0:T(8,128)(2,1)}, bf16[2,512,128]{2,1,0:T(8,128)(2,1)S(1)}, u32[]{:S(2)}, u32[]{:S(2)}) %collective-permute-start.1) | collective-permute-done | bytes 262176 | tf_op jit(solution)/shard_map/ppermute | solution.py:252
  27.0 0.0 collective-permute-start.2
  27.0 0.0 collective-permute-done.3.kv1
  27.0 0.5 collective-permute-start.4
  27.5 1.3 %collective-permute-done.5.kv1 = bf16[2,512,128]{2,1,0:T(8,128)(2,1)S(1)} collective-permute-done((bf16[2,512,128]{2,1,0:T(8,128)(2,1)}, bf16[2,512,128]{2,1,0:T(8,128)(2,1)S(1)}, u32[]{:S(2)}, u32[]{:S(2)}) %collective-permute-start.5) | collective-permute-done | bytes 262176 | tf_op jit(solution)/shard_map/ppermute | solution.py:252
  28.8 0.0 collective-permute-start.6
  28.8 0.0 copy-done.1
  28.8 0.7 broadcast_in_dim.2
  29.6 8.0 %all-to-all-start = ((bf16[16,8,1024]{2,1,0:T(8,128)(2,1)}), bf16[16,8,1024]{2,1,0:T(8,128)(2,1)S(1)}, u32[]{:S(2)}, u32[]{:S(2)}) async-start(bf16[16,8,1024]{2,1,0:T(8,128)(2,1)} %broadcast_in_dim.2), calls=%async_computation | async-start | bytes 524288 | tf_op jit(solution)/shard_map/all_to_all | solution.py:243
  37.6 0.0 copy-done
  37.6 0.5 collective-permute-start.7
  38.1 8.7 %all-to-all-done.q = bf16[16,8,1024]{2,1,0:T(8,128)(2,1)S(1)} async-done(((bf16[16,8,1024]{2,1,0:T(8,128)(2,1)}), bf16[16,8,1024]{2,1,0:T(8,128)(2,1)S(1)}, u32[]{:S(2)}, u32[]{:S(2)}) %all-to-all-start) | async-done | bytes 262176 | tf_op jit(solution)/shard_map/all_to_all | solution.py:243
  46.8 0.0 collective-permute-done.kv2
  46.8 1.7 %attend.4.refs_0_ = bf16[16,9,8,128]{3,2,1,0:T(8,128)(2,1)S(1)} custom-call(bf16[16,8,1024]{2,1,0:T(8,128)(2,1)S(1)} %all-to-all-done.q, bf16[2,512,128]{2,1,0:T(8,128)(2,1)S(1)} %get-tuple-element.10.kv1, bf16[2,512,128]{2,1,0:T(8,128)(2,1)S(1)} %collective-permute-done.kv2), custom_call_target="tpu_custom_call" | custom-call | tf_op jit(solution)/shard_map/attend/pallas_call | solution.py:144
  48.6 0.0 collective-permute-done.2.kv2
  48.6 1.7 %attend.5.refs_1_ = bf16[16,9,8,128]{3,2,1,0:T(8,128)(2,1)S(1)} custom-call(bf16[16,8,1024]{2,1,0:T(8,128)(2,1)S(1)} %all-to-all-done.q, bf16[2,512,128]{2,1,0:T(8,128)(2,1)S(1)} %collective-permute-done.1.kv1, bf16[2,512,128]{2,1,0:T(8,128)(2,1)S(1)} %collective-permute-done.2.kv2), custom_call_target="tpu_custom_call" | custom-call | tf_op jit(solution)/shard_map/attend/pallas_call | solution.py:144
  50.3 0.0 collective-permute-done.4.kv2
  50.3 1.7 %attend.6.refs_2_ = bf16[16,9,8,128]{3,2,1,0:T(8,128)(2,1)S(1)} custom-call(bf16[16,8,1024]{2,1,0:T(8,128)(2,1)S(1)} %all-to-all-done.q, bf16[2,512,128]{2,1,0:T(8,128)(2,1)S(1)} %collective-permute-done.3.kv1, bf16[2,512,128]{2,1,0:T(8,128)(2,1)S(1)} %collective-permute-done.4.kv2), custom_call_target="tpu_custom_call" | custom-call | tf_op jit(solution)/shard_map/attend/pallas_call | solution.py:144
  52.1 0.0 collective-permute-done.6.kv2
  52.1 1.7 %attend.7.refs_3_ = bf16[16,9,8,128]{3,2,1,0:T(8,128)(2,1)S(1)} custom-call(bf16[16,8,1024]{2,1,0:T(8,128)(2,1)S(1)} %all-to-all-done.q, bf16[2,512,128]{2,1,0:T(8,128)(2,1)S(1)} %collective-permute-done.5.kv1, bf16[2,512,128]{2,1,0:T(8,128)(2,1)S(1)} %collective-permute-done.6.kv2), custom_call_target="tpu_custom_call" | custom-call | tf_op jit(solution)/shard_map/attend/pallas_call | solution.py:144
  53.8 0.9 merge.1
  54.7 12.1 %all_to_all.20.parts = bf16[16,9,8,128]{3,2,1,0:T(8,128)(2,1)S(1)} all-to-all(bf16[16,9,8,128]{3,2,1,0:T(8,128)(2,1)S(1)} %merge.1), channel_id=1, replica_groups=mesh['y'=4,'z'=4,'core'=2,'head'=4] {'y','z'}, dimensions={0} | all-to-all | bytes 589824 | tf_op jit(solution)/shard_map/all_to_all | solution.py:243
  66.8 1.1 %combine.1 = bf16[16,8,1024]{2,1,0:T(8,128)(2,1)} custom-call(bf16[16,9,8,128]{3,2,1,0:T(8,128)(2,1)S(1)} %all_to_all.20.parts), custom_call_target="tpu_custom_call" | custom-call | tf_op jit(solution)/shard_map/combine/pallas_call | solution.py:208
  67.9 3.6 %all-to-all-start.2 = ((bf16[16,8,1024]{2,1,0:T(8,128)(2,1)}), bf16[16,8,1024]{2,1,0:T(8,128)(2,1)S(1)}, u32[]{:S(2)}, u32[]{:S(2)}) async-start(bf16[16,8,1024]{2,1,0:T(8,128)(2,1)} %combine.1), calls=%async_computation.2 | async-start | bytes 524288 | tf_op jit(solution)/shard_map/all_to_all | solution.py:243
  71.6 0.0 collective-permute-done.7.other
  71.6 8.5 %all-to-all-done.2.rows = bf16[16,8,1024]{2,1,0:T(8,128)(2,1)S(1)} async-done(((bf16[16,8,1024]{2,1,0:T(8,128)(2,1)}), bf16[16,8,1024]{2,1,0:T(8,128)(2,1)S(1)}, u32[]{:S(2)}, u32[]{:S(2)}) %all-to-all-start.2) | async-done | bytes 262176 | tf_op jit(solution)/shard_map/all_to_all | solution.py:243
  80.1 0.3 mix.1
  80.4 9.6 %all_to_all.21 = bf16[8,32,256]{2,1,0:T(8,128)(2,1)S(1)} all-to-all(bf16[8,32,256]{2,1,0:T(8,128)(2,1)S(1)} %bitcast.6), channel_id=1, replica_groups=mesh['y'=4,'z'=4,'core'=2,'head'=4] {'head','core'}, dimensions={0} | all-to-all | bytes 262144 | tf_op jit(solution)/shard_map/all_to_all | solution.py:243
  90.0 0.6 copy.6
  (1 shorter events, 0.0 us)
Async XLA Ops:
  0.0 28.8 %copy-start.1 = (bf16[8,1024]{1,0:T(8,128)(2,1)S(1)}, bf16[8,1024]{1,0:T(8,128)(2,1)}, u32[]{:S(2)}) copy-start(bf16[8,1024]{1,0:T(8,128)(2,1)} %param.8) | copy-start | bytes 49156
  0.0 37.6 %copy-start = (bf16[1024,256]{1,0:T(8,128)(2,1)S(1)}, bf16[1024,256]{1,0:T(8,128)(2,1)}, u32[]{:S(2)}) copy-start(bf16[1024,256]{1,0:T(8,128)(2,1)} %own.1) | copy-start | bytes 1572868
  12.5 14.6 %collective-permute-start.1 = (bf16[2,512,128]{2,1,0:T(8,128)(2,1)}, bf16[2,512,128]{2,1,0:T(8,128)(2,1)S(1)}, u32[]{:S(2)}, u32[]{:S(2)}) collective-permute-start(bf16[2,512,128]{2,1,0:T(8,128)(2,1)} %get-tuple-element.12), channel_id=1, source_target_pairs={{0,3},{1,0},{2,1},{3,2},{4,5},{5,6},{6,7},{7,4},{8,11},{9,8},{10,9... | collective-permute-start | bytes 786440 | tf_op jit(solution)/shard_map/ppermute | solution.py:252
  15.4 11.6 %collective-permute-start.3 = (bf16[2,512,128]{2,1,0:T(8,128)(2,1)}, bf16[2,512,128]{2,1,0:T(8,128)(2,1)S(1)}, u32[]{:S(2)}, u32[]{:S(2)}) collective-permute-start(bf16[2,512,128]{2,1,0:T(8,128)(2,1)} %get-tuple-element.13), channel_id=1, source_target_pairs={{0,1},{1,2},{2,3},{3,0},{4,7},{5,4},{6,5},{7,6},{8,9},{9,10},{10,1... | collective-permute-start | bytes 786440 | tf_op jit(solution)/shard_map/ppermute | solution.py:252
  15.4 13.4 %collective-permute-start.5 = (bf16[2,512,128]{2,1,0:T(8,128)(2,1)}, bf16[2,512,128]{2,1,0:T(8,128)(2,1)S(1)}, u32[]{:S(2)}, u32[]{:S(2)}) collective-permute-start(bf16[2,512,128]{2,1,0:T(8,128)(2,1)} %get-tuple-element.14), channel_id=1, source_target_pairs={{0,2},{1,3},{2,0},{3,1},{4,6},{5,7},{6,4},{7,5},{8,10},{9,11},{10,... | collective-permute-start | bytes 786440 | tf_op jit(solution)/shard_map/ppermute | solution.py:252
  17.7 29.1 %collective-permute-start = (bf16[2,512,128]{2,1,0:T(8,128)(2,1)}, bf16[2,512,128]{2,1,0:T(8,128)(2,1)S(1)}, u32[]{:S(2)}, u32[]{:S(2)}) collective-permute-start(bf16[2,512,128]{2,1,0:T(8,128)(2,1)} %get-tuple-element.11), channel_id=1, source_target_pairs={{0,4},{4,0},{1,5},{5,1},{2,6},{6,2},{3,7},{7,3},{8,12},{12,8},{9,1... | collective-permute-start | bytes 786440 | tf_op jit(solution)/shard_map/ppermute | solution.py:239
  27.0 21.5 %collective-permute-start.2 = (bf16[2,512,128]{2,1,0:T(8,128)(2,1)S(1)}, bf16[2,512,128]{2,1,0:T(8,128)(2,1)S(1)}, u32[]{:S(2)}, u32[]{:S(2)}) collective-permute-start(bf16[2,512,128]{2,1,0:T(8,128)(2,1)S(1)} %collective-permute-done.1.kv1), channel_id=1, source_target_pairs={{0,4},{4,0},{1,5},{5,1},{2,6},{6,2},{3,7},{7,3},{8,12},{12,8},{9,1... | collective-permute-start | bytes 786440 | tf_op jit(solution)/shard_map/ppermute | solution.py:239
  27.0 23.3 %collective-permute-start.4 = (bf16[2,512,128]{2,1,0:T(8,128)(2,1)S(1)}, bf16[2,512,128]{2,1,0:T(8,128)(2,1)S(1)}, u32[]{:S(2)}, u32[]{:S(2)}) collective-permute-start(bf16[2,512,128]{2,1,0:T(8,128)(2,1)S(1)} %collective-permute-done.3.kv1), channel_id=1, source_target_pairs={{0,4},{4,0},{1,5},{5,1},{2,6},{6,2},{3,7},{7,3},{8,12},{12,8},{9,1... | collective-permute-start | bytes 786440 | tf_op jit(solution)/shard_map/ppermute | solution.py:239
  28.8 23.3 %collective-permute-start.6 = (bf16[2,512,128]{2,1,0:T(8,128)(2,1)S(1)}, bf16[2,512,128]{2,1,0:T(8,128)(2,1)S(1)}, u32[]{:S(2)}, u32[]{:S(2)}) collective-permute-start(bf16[2,512,128]{2,1,0:T(8,128)(2,1)S(1)} %collective-permute-done.5.kv1), channel_id=1, source_target_pairs={{0,4},{4,0},{1,5},{5,1},{2,6},{6,2},{3,7},{7,3},{8,12},{12,8},{9,1... | collective-permute-start | bytes 786440 | tf_op jit(solution)/shard_map/ppermute | solution.py:239
  29.6 17.2 %all-to-all-start = ((bf16[16,8,1024]{2,1,0:T(8,128)(2,1)}), bf16[16,8,1024]{2,1,0:T(8,128)(2,1)S(1)}, u32[]{:S(2)}, u32[]{:S(2)}) async-start(bf16[16,8,1024]{2,1,0:T(8,128)(2,1)} %broadcast_in_dim.2), calls=%async_computation | async-start | bytes 524288 | tf_op jit(solution)/shard_map/all_to_all | solution.py:243
  37.6 34.0 %collective-permute-start.7 = (bf16[1024,256]{1,0:T(8,128)(2,1)S(1)}, bf16[1024,256]{1,0:T(8,128)(2,1)S(1)}, u32[]{:S(2)}, u32[]{:S(2)}) collective-permute-start(bf16[1024,256]{1,0:T(8,128)(2,1)S(1)} %copy-done), channel_id=1, source_target_pairs={{0,4},{4,0},{1,5},{5,1},{2,6},{6,2},{3,7},{7,3},{8,12},{12,8},{9,1... | collective-permute-start | bytes 1572872 | tf_op jit(solution)/shard_map/ppermute | solution.py:239
  67.9 12.1 %all-to-all-start.2 = ((bf16[16,8,1024]{2,1,0:T(8,128)(2,1)}), bf16[16,8,1024]{2,1,0:T(8,128)(2,1)S(1)}, u32[]{:S(2)}, u32[]{:S(2)}) async-start(bf16[16,8,1024]{2,1,0:T(8,128)(2,1)} %combine.1), calls=%async_computation.2 | async-start | bytes 524288 | tf_op jit(solution)/shard_map/all_to_all | solution.py:243

commit v5 on v4

--- a/solution.py
+++ b/solution.py
@@ -23,7 +23,7 @@
 YZ = ("y", "z")
 CHUNKS = (768,) * 10
 AHEAD = 3
-AHEADS = (0, 0, 2, 1, -1)
+AHEADS = (0, 2, 1, -1)
 
 
 def limit(mib):
@@ -78,8 +78,7 @@
         project_kernel,
         in_specs=[SMEM] * 2 + [HBM] * 3,
         out_specs=[VMEM] * len(AHEADS),
-        out_shape=[pltpu.VMEM((2, rows, HD), jnp.bfloat16)]
-        + [jax.ShapeDtypeStruct((2, rows, HD), jnp.bfloat16)] * GROUPS,
+        out_shape=[pltpu.VMEM((2, rows, HD), jnp.bfloat16)] * len(AHEADS),
         scratch_shapes=[
             pltpu.VMEM((rows, width), jnp.bfloat16),
             pltpu.VMEM((width, cols), jnp.bfloat16),
@@ -106,30 +105,31 @@
     return tile.astype(jnp.bfloat16)
 
 
-def attend_kernel(q, kv1, kv2, out):
-    tokens = kv1.shape[1]
+def attend_kernel(q, *rest):
+    kvs, out = rest[:-1], rest[-1]
     row = lax.broadcasted_iota(jnp.int32, (ROWS, HD), 0)
     lane = lax.broadcasted_iota(jnp.int32, (ROWS, HD), 1)
     contract = (((1,), (1,)), ((), ()))
-    ones = jnp.ones((tokens, HD), jnp.bfloat16)
-    k1, k2 = kv1[0], kv2[0]
-    v1 = jnp.concatenate([kv1[1], ones], axis=1)
-    v2 = jnp.concatenate([kv2[1], ones], axis=1)
+    ones = jnp.ones(kvs[0].shape[1:], jnp.bfloat16)
+    values = [jnp.concatenate([kv[1], ones], axis=1) for kv in kvs]
     stats = jnp.zeros((ROWS, HD), jnp.float32)
     for first in range(0, HEADS, STACK):
         qs = [
-            q[:, :, h * HD : (h + 1) * HD].reshape(ROWS, HD)
-            for h in range(first, first + STACK)
+            q[:, :, h * HD : (h + 1) * HD].reshape(ROWS, HD) for h in range(first, first + STACK)
         ]
         qs = jnp.concatenate(qs, axis=0)
-        s1 = lax.dot_general(qs, k1, contract, preferred_element_type=jnp.float32)
-        s2 = lax.dot_general(qs, k2, contract, preferred_element_type=jnp.float32)
-        top = jnp.max(jnp.maximum(s1, s2), axis=1, keepdims=True)
-        p1 = jnp.exp2((s1 - top) * EXP2_SCALE).astype(jnp.bfloat16)
-        p2 = jnp.exp2((s2 - top) * EXP2_SCALE).astype(jnp.bfloat16)
-        acc = jnp.dot(p1, v1, preferred_element_type=jnp.float32) + jnp.dot(
-            p2, v2, preferred_element_type=jnp.float32
-        )
+        scores = [
+            lax.dot_general(qs, kv[0], contract, preferred_element_type=jnp.float32)
+            for kv in kvs
+        ]
+        top = scores[0]
+        for s in scores[1:]:
+            top = jnp.maximum(top, s)
+        top = jnp.max(top, axis=1, keepdims=True)
+        acc = jnp.zeros((STACK * ROWS, 2 * HD), jnp.float32)
+        for s, v in zip(scores, values):
+            p = jnp.exp2((s - top) * EXP2_SCALE).astype(jnp.bfloat16)
+            acc = acc + jnp.dot(p, v, preferred_element_type=jnp.float32)
         for k in range(STACK):
             h = first + k
             mine = acc[k * ROWS : (k + 1) * ROWS]
@@ -140,15 +140,15 @@
     out[:, HEADS] = stats_tile(jnp.sum(stats.reshape(PEERS, RPD, HD), axis=1))
 
 
-def attend(q, kv1, kv2):
+def attend(q, kvs):
     return pl.pallas_call(
         attend_kernel,
-        in_specs=[VMEM] * 3,
+        in_specs=[VMEM] * (1 + len(kvs)),
         out_specs=VMEM,
         out_shape=jax.ShapeDtypeStruct((PEERS, BLK, RPD, HD), jnp.bfloat16),
-        compiler_params=limit(24),
+        compiler_params=limit(40),
         name="attend",
-    )(q, kv1, kv2)
+    )(q, *kvs)
 
 
 def read_stats(part):
@@ -235,6 +235,28 @@
     )(core, rows, own, other)
 
 
+def total_kernel(shares, out):
+    total = shares[0].astype(jnp.float32)
+    for g in range(1, GROUPS):
+        total = total + shares[g].astype(jnp.float32)
+    cols = out.shape[1]
+    total = total.reshape(2, GROUPS, RPD, cols)
+    pair = jnp.concatenate([total[0][:, None], total[1][:, None]], axis=1)
+    out[...] = pair.reshape(2 * GROUPS * RPD, cols).astype(jnp.bfloat16)
+
+
+def total_of(shares):
+    rows, cols = shares.shape[1:]
+    return pl.pallas_call(
+        total_kernel,
+        in_specs=[VMEM],
+        out_specs=VMEM,
+        out_shape=jax.ShapeDtypeStruct((rows, cols), jnp.bfloat16),
+        compiler_params=limit(4),
+        name="total",
+    )(shares)
+
+
 def swap_cores(x):
     return lax.ppermute(x, "core", [(0, 1), (1, 0)])
 
@@ -260,23 +282,20 @@
     copies = jnp.broadcast_to(queries[None], (PEERS,) + queries.shape)
     rows = exchange(copies, YZ)
     head, core = index_of("head"), index_of("core")
-    own, twin, far, near, back = project(head, 2 * core - 1, vision, w_key, w_value)
+    own, far, near, back = project(head, 2 * core - 1, vision, w_key, w_value)
     far = send_block(far, 2)
     near = send_block(near, 1)
     back = send_block(back, -1)
-    parts = [
-        attend(rows, kv, swap_cores(sent))
-        for kv, sent in ((own, twin), (near, near), (back, back), (far, far))
-    ]
-    part = merge(parts)
+    part_own = attend(rows, [own, swap_cores(own)])
+    others = [near, back, far]
+    others += [swap_cores(near), swap_cores(back), swap_cores(far)]
+    part = merge([part_own, attend(rows, others)])
     w_other = swap_cores(w_out)
     attended = exchange(combine(exchange(part, YZ)), YZ)
     partial = mix(core, attended, w_out, w_other)
     shape = partial.shape[2:]
     shares = exchange(partial.reshape((-1,) + shape), ("head", "core"))
-    shares = shares.reshape(GROUPS, 2, GROUPS, RPD, -1).astype(jnp.float32)
-    total = jnp.sum(shares, axis=0).transpose(1, 0, 2, 3)
-    return total.reshape(2 * GROUPS * RPD, -1).astype(jnp.bfloat16)
+    return total_of(shares.reshape(GROUPS, 2 * GROUPS * RPD, -1))
 
 
 def solution(mesh):

time: 91.5 us -> 89.2 us (0.975)
  Pallas kernels: 21.7 us -> 20.2 us
    pallas_call x1, Pallas kernels: 12.5 us -> 11.4 us  [project(): pl.pallas_call(project_kernel, in_specs=[SMEM] * 2 + [HBM] * 3, out_specs...]
    pallas_call x4 -> x3, Pallas kernels: 6.97 us -> 6.94 us  [the longest x2 6.31 us: attend(): pl.pallas_call(attend_kernel, in_specs=[VMEM] * (1 + len(kvs)), out_specs...]
  transfers between devices with their start and end apart: 10 -> 10, of which waited for: 4 -> 4; matrix products, arithmetic and copies ran while one was open for 1% -> 1% of each run, Pallas kernels for 10% -> 9%
where the time goes in v5:
time: 89.2 us; the launch traced here: 88.2 us
  waiting for transfers between devices  27.5 us (31%)
  blocking collectives  21.7 us (24%)
  Pallas kernels  20.2 us (23%)
  starting transfers between devices  17.9 us (20%)
    all_to_all x2, blocking collectives, exchange(): return lax.all_to_all(x, axes, split_axis=0, concat_axis=0, tiled=True)  21.7 us
    all_to_all x2, waiting for transfers between devices, exchange(): return lax.all_to_all(x, axes, split_axis=0, concat_axis=0, tiled=True)  17.1 us
    all_to_all x2, starting transfers between devices, exchange(): return lax.all_to_all(x, axes, split_axis=0, concat_axis=0, tiled=True)  11.7 us
    pallas_call x1, Pallas kernels, project(): pl.pallas_call(project_kernel, in_specs=[SMEM] * 2 + [HBM] * 3, out_specs...  11.4 us
    ppermute x3, waiting for transfers between devices, send_block(): return lax.ppermute(x, ('core', 'head'), pairs)  10.4 us
    pallas_call x2, Pallas kernels, attend(): pl.pallas_call(attend_kernel, in_specs=[VMEM] * (1 + len(kvs)), out_specs...  6.31 us
    ppermute x3, starting transfers between devices, send_block(): return lax.ppermute(x, ('core', 'head'), pairs)  5.23 us
  transfers between devices with their start and end apart: 10, of which 4 were waited for; matrix products, arithmetic and copies ran while one was open for 1% of the time, Pallas kernels for 9%

profile of v5, /device:TPU:0, one launch (start us, length us, event | category | flops | bytes accessed | tf_op | source)
XLA Modules:
  0.0 88.2 jit_solution(4776672606507926726)
XLA Ops:
  0.0 0.0 copy-start.1
  0.0 0.0 copy-start
  0.0 11.4 %project.1 = (bf16[2,512,128]{2,1,0:T(8,128)(2,1)S(1)}, bf16[2,512,128]{2,1,0:T(8,128)(2,1)S(1)}, bf16[2,512,128]{2,1,0:T(8,128)(2,1)S(1)}, bf16[2,512,128]{2,1,0:T(8,128)(2,1)S(1)}) custom-call(s32[1]{0:T(128)} %bitcast.1.head, s32[1]{0:T(128)S(6)} %sub.3.way, bf16[512,7680]{1,0:T(8,128)(2,1)} %x.1, bf16[7680,512]{1,0:T(8,128)(2,1)} %wk.1, bf16[7680,512]{1,0:T(8,128)(2,1)} %wv.1), custom_call_target="tpu_custom_call" | custom-call | tf_op jit(solution)/shard_map/project/pallas_call | solution.py:77
  11.4 2.9 %collective-permute-start.1 = (bf16[2,512,128]{2,1,0:T(8,128)(2,1)S(1)}, bf16[2,512,128]{2,1,0:T(8,128)(2,1)S(1)}, u32[]{:S(2)}, u32[]{:S(2)}) collective-permute-start(bf16[2,512,128]{2,1,0:T(8,128)(2,1)S(1)} %get-tuple-element.10), channel_id=1, source_target_pairs={{0,3},{1,0},{2,1},{3,2},{4,5},{5,6},{6,7},{7,4},{8,11},{9,8},{10,9... | collective-permute-start | bytes 786440 | tf_op jit(solution)/shard_map/ppermute | solution.py:274
  14.3 0.0 collective-permute-start.2
  14.3 2.3 %collective-permute-start.3 = (bf16[2,512,128]{2,1,0:T(8,128)(2,1)S(1)}, bf16[2,512,128]{2,1,0:T(8,128)(2,1)S(1)}, u32[]{:S(2)}, u32[]{:S(2)}) collective-permute-start(bf16[2,512,128]{2,1,0:T(8,128)(2,1)S(1)} %get-tuple-element.12), channel_id=1, source_target_pairs={{0,2},{1,3},{2,0},{3,1},{4,6},{5,7},{6,4},{7,5},{8,10},{9,11},{10,... | collective-permute-start | bytes 786440 | tf_op jit(solution)/shard_map/ppermute | solution.py:274
  16.6 0.0 collective-permute-start
  16.6 9.0 %collective-permute-done.1.rest_0_ = bf16[2,512,128]{2,1,0:T(8,128)(2,1)S(1)} collective-permute-done((bf16[2,512,128]{2,1,0:T(8,128)(2,1)S(1)}, bf16[2,512,128]{2,1,0:T(8,128)(2,1)S(1)}, u32[]{:S(2)}, u32[]{:S(2)}) %collective-permute-start.1) | collective-permute-done | bytes 262176 | tf_op jit(solution)/shard_map/ppermute | solution.py:274
  25.6 0.0 collective-permute-start.4
  25.6 0.0 collective-permute-done.2.rest_1_
  25.6 0.5 collective-permute-start.5
  26.1 1.4 %collective-permute-done.3.rest_2_ = bf16[2,512,128]{2,1,0:T(8,128)(2,1)S(1)} collective-permute-done((bf16[2,512,128]{2,1,0:T(8,128)(2,1)S(1)}, bf16[2,512,128]{2,1,0:T(8,128)(2,1)S(1)}, u32[]{:S(2)}, u32[]{:S(2)}) %collective-permute-start.3) | collective-permute-done | bytes 262176 | tf_op jit(solution)/shard_map/ppermute | solution.py:274
  27.5 0.0 collective-permute-start.6
  27.5 0.0 copy-done.1
  27.5 0.7 broadcast_in_dim.2
  28.2 8.0 %all-to-all-start = ((bf16[16,8,1024]{2,1,0:T(8,128)(2,1)}), bf16[16,8,1024]{2,1,0:T(8,128)(2,1)S(1)}, u32[]{:S(2)}, u32[]{:S(2)}) async-start(bf16[16,8,1024]{2,1,0:T(8,128)(2,1)} %broadcast_in_dim.2), calls=%async_computation | async-start | bytes 524288 | tf_op jit(solution)/shard_map/all_to_all | solution.py:265
  36.3 0.0 copy-done
  36.3 0.5 collective-permute-start.7
  36.8 8.7 %all-to-all-done.q = bf16[16,8,1024]{2,1,0:T(8,128)(2,1)S(1)} async-done(((bf16[16,8,1024]{2,1,0:T(8,128)(2,1)}), bf16[16,8,1024]{2,1,0:T(8,128)(2,1)S(1)}, u32[]{:S(2)}, u32[]{:S(2)}) %all-to-all-start) | async-done | bytes 262176 | tf_op jit(solution)/shard_map/all_to_all | solution.py:265
  45.5 0.0 collective-permute-done.rest_1_
  45.5 1.7 %attend.2.refs_0_ = bf16[16,9,8,128]{3,2,1,0:T(8,128)(2,1)S(1)} custom-call(bf16[16,8,1024]{2,1,0:T(8,128)(2,1)S(1)} %all-to-all-done.q, bf16[2,512,128]{2,1,0:T(8,128)(2,1)S(1)} %get-tuple-element.9.rest_0_, bf16[2,512,128]{2,1,0:T(8,128)(2,1)S(1)} %collective-permute-done.rest_1_), custom_call_target="tpu_custom_call" | custom-call | tf_op jit(solution)/shard_map/attend/pallas_call | solution.py:144
  47.2 0.0 collective-permute-done.4.rest_3_
  47.2 0.0 collective-permute-done.5.rest_4_
  47.2 0.0 collective-permute-done.6.rest_5_
  47.3 4.6 %attend.3.refs_1_ = bf16[16,9,8,128]{3,2,1,0:T(8,128)(2,1)S(1)} custom-call(bf16[16,8,1024]{2,1,0:T(8,128)(2,1)S(1)} %all-to-all-done.q, bf16[2,512,128]{2,1,0:T(8,128)(2,1)S(1)} %collective-permute-done.1.rest_0_, bf16[2,512,128]{2,1,0:T(8,128)(2,1)S(1)} %collective-permute-done.2.rest_1_, bf16[2,512,128]{2,1,0:T(8,128)(2,1)S(1)} %collective-permute-done.3.rest_2_, ...), custom_call_target="tpu_custom_call" | custom-call | tf_op jit(solution)/shard_map/attend/pallas_call | solution.py:144
  51.8 0.5 merge.1
  52.3 12.1 %all_to_all.20.parts = bf16[16,9,8,128]{3,2,1,0:T(8,128)(2,1)S(1)} all-to-all(bf16[16,9,8,128]{3,2,1,0:T(8,128)(2,1)S(1)} %merge.1), channel_id=1, replica_groups=mesh['y'=4,'z'=4,'core'=2,'head'=4] {'y','z'}, dimensions={0} | all-to-all | bytes 589824 | tf_op jit(solution)/shard_map/all_to_all | solution.py:265
  64.4 1.1 %combine.1 = bf16[16,8,1024]{2,1,0:T(8,128)(2,1)} custom-call(bf16[16,9,8,128]{3,2,1,0:T(8,128)(2,1)S(1)} %all_to_all.20.parts), custom_call_target="tpu_custom_call" | custom-call | tf_op jit(solution)/shard_map/combine/pallas_call | solution.py:208
  65.6 3.6 %all-to-all-start.2 = ((bf16[16,8,1024]{2,1,0:T(8,128)(2,1)}), bf16[16,8,1024]{2,1,0:T(8,128)(2,1)S(1)}, u32[]{:S(2)}, u32[]{:S(2)}) async-start(bf16[16,8,1024]{2,1,0:T(8,128)(2,1)} %combine.1), calls=%async_computation.2 | async-start | bytes 524288 | tf_op jit(solution)/shard_map/all_to_all | solution.py:265
  69.2 0.0 collective-permute-done.7.other
  69.2 8.5 %all-to-all-done.2.rows = bf16[16,8,1024]{2,1,0:T(8,128)(2,1)S(1)} async-done(((bf16[16,8,1024]{2,1,0:T(8,128)(2,1)}), bf16[16,8,1024]{2,1,0:T(8,128)(2,1)S(1)}, u32[]{:S(2)}, u32[]{:S(2)}) %all-to-all-start.2) | async-done | bytes 262176 | tf_op jit(solution)/shard_map/all_to_all | solution.py:265
  77.7 0.3 mix.1
  78.0 9.6 %all_to_all.21 = bf16[8,32,256]{2,1,0:T(8,128)(2,1)S(1)} all-to-all(bf16[8,32,256]{2,1,0:T(8,128)(2,1)S(1)} %bitcast.5), channel_id=1, replica_groups=mesh['y'=4,'z'=4,'core'=2,'head'=4] {'head','core'}, dimensions={0} | all-to-all | bytes 262144 | tf_op jit(solution)/shard_map/all_to_all | solution.py:265
  87.6 0.6 total.1
Async XLA Ops:
  0.0 27.5 %copy-start.1 = (bf16[8,1024]{1,0:T(8,128)(2,1)S(1)}, bf16[8,1024]{1,0:T(8,128)(2,1)}, u32[]{:S(2)}) copy-start(bf16[8,1024]{1,0:T(8,128)(2,1)} %param.8) | copy-start | bytes 49156
  0.0 36.3 %copy-start = (bf16[1024,256]{1,0:T(8,128)(2,1)S(1)}, bf16[1024,256]{1,0:T(8,128)(2,1)}, u32[]{:S(2)}) copy-start(bf16[1024,256]{1,0:T(8,128)(2,1)} %own.1) | copy-start | bytes 1572868
  11.4 14.2 %collective-permute-start.1 = (bf16[2,512,128]{2,1,0:T(8,128)(2,1)S(1)}, bf16[2,512,128]{2,1,0:T(8,128)(2,1)S(1)}, u32[]{:S(2)}, u32[]{:S(2)}) collective-permute-start(bf16[2,512,128]{2,1,0:T(8,128)(2,1)S(1)} %get-tuple-element.10), channel_id=1, source_target_pairs={{0,3},{1,0},{2,1},{3,2},{4,5},{5,6},{6,7},{7,4},{8,11},{9,8},{10,9... | collective-permute-start | bytes 786440 | tf_op jit(solution)/shard_map/ppermute | solution.py:274
  14.3 11.3 %collective-permute-start.2 = (bf16[2,512,128]{2,1,0:T(8,128)(2,1)S(1)}, bf16[2,512,128]{2,1,0:T(8,128)(2,1)S(1)}, u32[]{:S(2)}, u32[]{:S(2)}) collective-permute-start(bf16[2,512,128]{2,1,0:T(8,128)(2,1)S(1)} %get-tuple-element.11), channel_id=1, source_target_pairs={{0,1},{1,2},{2,3},{3,0},{4,7},{5,4},{6,5},{7,6},{8,9},{9,10},{10,1... | collective-permute-start | bytes 786440 | tf_op jit(solution)/shard_map/ppermute | solution.py:274
  14.3 13.2 %collective-permute-start.3 = (bf16[2,512,128]{2,1,0:T(8,128)(2,1)S(1)}, bf16[2,512,128]{2,1,0:T(8,128)(2,1)S(1)}, u32[]{:S(2)}, u32[]{:S(2)}) collective-permute-start(bf16[2,512,128]{2,1,0:T(8,128)(2,1)S(1)} %get-tuple-element.12), channel_id=1, source_target_pairs={{0,2},{1,3},{2,0},{3,1},{4,6},{5,7},{6,4},{7,5},{8,10},{9,11},{10,... | collective-permute-start | bytes 786440 | tf_op jit(solution)/shard_map/ppermute | solution.py:274
  16.6 28.9 %collective-permute-start = (bf16[2,512,128]{2,1,0:T(8,128)(2,1)S(1)}, bf16[2,512,128]{2,1,0:T(8,128)(2,1)S(1)}, u32[]{:S(2)}, u32[]{:S(2)}) collective-permute-start(bf16[2,512,128]{2,1,0:T(8,128)(2,1)S(1)} %get-tuple-element.9.rest_0_), channel_id=1, source_target_pairs={{0,4},{4,0},{1,5},{5,1},{2,6},{6,2},{3,7},{7,3},{8,12},{12,8},{9,1... | collective-permute-start | bytes 786440 | tf_op jit(solution)/shard_map/ppermute | solution.py:261
  25.6 21.6 %collective-permute-start.4 = (bf16[2,512,128]{2,1,0:T(8,128)(2,1)S(1)}, bf16[2,512,128]{2,1,0:T(8,128)(2,1)S(1)}, u32[]{:S(2)}, u32[]{:S(2)}) collective-permute-start(bf16[2,512,128]{2,1,0:T(8,128)(2,1)S(1)} %collective-permute-done.1.rest_0_), channel_id=1, source_target_pairs={{0,4},{4,0},{1,5},{5,1},{2,6},{6,2},{3,7},{7,3},{8,12},{12,8},{9,1... | collective-permute-start | bytes 786440 | tf_op jit(solution)/shard_map/ppermute | solution.py:261
  25.6 21.6 %collective-permute-start.5 = (bf16[2,512,128]{2,1,0:T(8,128)(2,1)S(1)}, bf16[2,512,128]{2,1,0:T(8,128)(2,1)S(1)}, u32[]{:S(2)}, u32[]{:S(2)}) collective-permute-start(bf16[2,512,128]{2,1,0:T(8,128)(2,1)S(1)} %collective-permute-done.2.rest_1_), channel_id=1, source_target_pairs={{0,4},{4,0},{1,5},{5,1},{2,6},{6,2},{3,7},{7,3},{8,12},{12,8},{9,1... | collective-permute-start | bytes 786440 | tf_op jit(solution)/shard_map/ppermute | solution.py:261
  27.5 19.7 %collective-permute-start.6 = (bf16[2,512,128]{2,1,0:T(8,128)(2,1)S(1)}, bf16[2,512,128]{2,1,0:T(8,128)(2,1)S(1)}, u32[]{:S(2)}, u32[]{:S(2)}) collective-permute-start(bf16[2,512,128]{2,1,0:T(8,128)(2,1)S(1)} %collective-permute-done.3.rest_2_), channel_id=1, source_target_pairs={{0,4},{4,0},{1,5},{5,1},{2,6},{6,2},{3,7},{7,3},{8,12},{12,8},{9,1... | collective-permute-start | bytes 786440 | tf_op jit(solution)/shard_map/ppermute | solution.py:261
  28.2 17.2 %all-to-all-start = ((bf16[16,8,1024]{2,1,0:T(8,128)(2,1)}), bf16[16,8,1024]{2,1,0:T(8,128)(2,1)S(1)}, u32[]{:S(2)}, u32[]{:S(2)}) async-start(bf16[16,8,1024]{2,1,0:T(8,128)(2,1)} %broadcast_in_dim.2), calls=%async_computation | async-start | bytes 524288 | tf_op jit(solution)/shard_map/all_to_all | solution.py:265
  36.3 32.9 %collective-permute-start.7 = (bf16[1024,256]{1,0:T(8,128)(2,1)S(1)}, bf16[1024,256]{1,0:T(8,128)(2,1)S(1)}, u32[]{:S(2)}, u32[]{:S(2)}) collective-permute-start(bf16[1024,256]{1,0:T(8,128)(2,1)S(1)} %copy-done), channel_id=1, source_target_pairs={{0,4},{4,0},{1,5},{5,1},{2,6},{6,2},{3,7},{7,3},{8,12},{12,8},{9,1... | collective-permute-start | bytes 1572872 | tf_op jit(solution)/shard_map/ppermute | solution.py:261
  65.6 12.1 %all-to-all-start.2 = ((bf16[16,8,1024]{2,1,0:T(8,128)(2,1)}), bf16[16,8,1024]{2,1,0:T(8,128)(2,1)S(1)}, u32[]{:S(2)}, u32[]{:S(2)}) async-start(bf16[16,8,1024]{2,1,0:T(8,128)(2,1)} %combine.1), calls=%async_computation.2 | async-start | bytes 524288 | tf_op jit(solution)/shard_map/all_to_all | solution.py:265

commit v6 on v5

--- a/solution.py
+++ b/solution.py
@@ -22,7 +22,7 @@
 SMEM = pl.BlockSpec(memory_space=pltpu.SMEM)
 YZ = ("y", "z")
 CHUNKS = (768,) * 10
-AHEAD = 3
+AHEAD = 10
 AHEADS = (0, 2, 1, -1)
 
 
@@ -105,87 +105,80 @@
     return tile.astype(jnp.bfloat16)
 
 
-def attend_kernel(q, *rest):
+def attend_heads(q, kvs, first):
+    contract = (((1,), (1,)), ((), ()))
+    qs = [q[:, :, h * HD : (h + 1) * HD].reshape(ROWS, HD) for h in range(first, first + STACK)]
+    qs = jnp.concatenate(qs, axis=0)
+    scores = [
+        lax.dot_general(qs, kv[0], contract, preferred_element_type=jnp.float32) for kv in kvs
+    ]
+    top = scores[0]
+    for s in scores[1:]:
+        top = jnp.maximum(top, s)
+    return scores, jnp.max(top, axis=1, keepdims=True)
+
+
+def weigh(scores, values, top, acc):
+    for s, v in zip(scores, values):
+        p = jnp.exp2((s - top) * EXP2_SCALE).astype(jnp.bfloat16)
+        acc = acc + jnp.dot(p, v, preferred_element_type=jnp.float32)
+    return acc
+
+
+def with_ones(kvs):
+    ones = jnp.ones(kvs[0].shape[1:], jnp.bfloat16)
+    return [jnp.concatenate([kv[1], ones], axis=1) for kv in kvs]
+
+
+def begin_kernel(q, *rest):
     kvs, out = rest[:-1], rest[-1]
+    values = with_ones(kvs)
+    shape = (STACK * ROWS, 2 * HD)
+    lane = lax.broadcasted_iota(jnp.int32, shape, 1)
+    for first in range(0, HEADS, STACK):
+        scores, top = attend_heads(q, kvs, first)
+        acc = weigh(scores, values, top, jnp.zeros(shape, jnp.float32))
+        out[first * ROWS : (first + STACK) * ROWS, :] = jnp.where(lane == 2 * HD - 1, top, acc)
+
+
+def finish_kernel(q, begun, *rest):
+    kvs, out = rest[:-1], rest[-1]
+    values = with_ones(kvs)
     row = lax.broadcasted_iota(jnp.int32, (ROWS, HD), 0)
     lane = lax.broadcasted_iota(jnp.int32, (ROWS, HD), 1)
-    contract = (((1,), (1,)), ((), ()))
-    ones = jnp.ones(kvs[0].shape[1:], jnp.bfloat16)
-    values = [jnp.concatenate([kv[1], ones], axis=1) for kv in kvs]
     stats = jnp.zeros((ROWS, HD), jnp.float32)
     for first in range(0, HEADS, STACK):
-        qs = [
-            q[:, :, h * HD : (h + 1) * HD].reshape(ROWS, HD) for h in range(first, first + STACK)
-        ]
-        qs = jnp.concatenate(qs, axis=0)
-        scores = [
-            lax.dot_general(qs, kv[0], contract, preferred_element_type=jnp.float32)
-            for kv in kvs
-        ]
-        top = scores[0]
-        for s in scores[1:]:
-            top = jnp.maximum(top, s)
-        top = jnp.max(top, axis=1, keepdims=True)
-        acc = jnp.zeros((STACK * ROWS, 2 * HD), jnp.float32)
-        for s, v in zip(scores, values):
-            p = jnp.exp2((s - top) * EXP2_SCALE).astype(jnp.bfloat16)
-            acc = acc + jnp.dot(p, v, preferred_element_type=jnp.float32)
+        before = begun[first * ROWS : (first + STACK) * ROWS, :]
+        top_before = before[:, 2 * HD - 1 :]
+        scores, top = attend_heads(q, kvs, first)
+        top = jnp.maximum(top, top_before)
+        acc = before * jnp.exp2((top_before - top) * EXP2_SCALE)
+        acc = weigh(scores, values, top, acc)
         for k in range(STACK):
             h = first + k
             mine = acc[k * ROWS : (k + 1) * ROWS]
+            sums = mine[:, HD : HD + 1]
             out[:, h] = mine[:, :HD].reshape(PEERS, RPD, HD).astype(jnp.bfloat16)
             pair = h * RPD + row % RPD
             stats = jnp.where(lane == pair, top[k * ROWS : (k + 1) * ROWS], stats)
-            stats = jnp.where(lane == HD // 2 + pair, mine[:, HD:], stats)
+            stats = jnp.where(lane == HD // 2 + pair, sums, stats)
     out[:, HEADS] = stats_tile(jnp.sum(stats.reshape(PEERS, RPD, HD), axis=1))
 
 
-def attend(q, kvs):
-    return pl.pallas_call(
-        attend_kernel,
-        in_specs=[VMEM] * (1 + len(kvs)),
+def attend(kernel, out_shape, q, arrays):
+    return pl.pallas_call(
+        kernel,
+        in_specs=[VMEM] * (1 + len(arrays)),
         out_specs=VMEM,
-        out_shape=jax.ShapeDtypeStruct((PEERS, BLK, RPD, HD), jnp.bfloat16),
+        out_shape=out_shape,
         compiler_params=limit(40),
         name="attend",
-    )(q, *kvs)
+    )(q, *arrays)
 
 
 def read_stats(part):
     stats = jnp.sum(part[:, HEADS].astype(jnp.float32), axis=1)
     return stats[:, : HD // 2], stats[:, HD // 2 :]
-
-
-def merge_kernel(*refs):
-    sources, out = refs[:-1], refs[-1]
-    stats = [read_stats(part) for part in sources]
-    top = stats[0][0]
-    for maxima, _ in stats[1:]:
-        top = jnp.maximum(top, maxima)
-    total = jnp.zeros_like(top)
-    weights = []
-    for maxima, sums in stats:
-        factor = jnp.exp2((maxima - top) * EXP2_SCALE)
-        total = total + factor * sums
-        weights.append(factor.T)
-    for p in range(PEERS):
-        acc = jnp.zeros((HEADS * RPD, HD), jnp.float32)
-        for part, weight in zip(sources, weights):
-            value = part[p, :HEADS].astype(jnp.float32).reshape(HEADS * RPD, HD)
-            acc = acc + value * weight[:, p : p + 1]
-        out[p, :HEADS] = acc.reshape(HEADS, RPD, HD).astype(jnp.bfloat16)
-    out[:, HEADS] = stats_tile(jnp.concatenate([top, total], axis=1))
-
-
-def merge(parts):
-    return pl.pallas_call(
-        merge_kernel,
-        in_specs=[VMEM] * len(parts),
-        out_specs=VMEM,
-        out_shape=jax.ShapeDtypeStruct((PEERS, BLK, RPD, HD), jnp.bfloat16),
-        compiler_params=limit(8),
-        name="merge",
-    )(*parts)
 
 
 def combine_kernel(parts, out):
@@ -286,10 +279,12 @@
     far = send_block(far, 2)
     near = send_block(near, 1)
     back = send_block(back, -1)
-    part_own = attend(rows, [own, swap_cores(own)])
+    begun = jax.ShapeDtypeStruct((HEADS * ROWS, 2 * HD), jnp.float32)
+    begun = attend(begin_kernel, begun, rows, [own, swap_cores(own)])
     others = [near, back, far]
     others += [swap_cores(near), swap_cores(back), swap_cores(far)]
-    part = merge([part_own, attend(rows, others)])
+    shape = jax.ShapeDtypeStruct((PEERS, BLK, RPD, HD), jnp.bfloat16)
+    part = attend(finish_kernel, shape, rows, [begun] + others)
     w_other = swap_cores(w_out)
     attended = exchange(combine(exchange(part, YZ)), YZ)
     partial = mix(core, attended, w_out, w_other)

time: 89.2 us -> 88.8 us (level)
    pallas_call x3 -> x2, Pallas kernels: 6.81 us -> 6.47 us  [attend(): pl.pallas_call(kernel, in_specs=[VMEM] * (1 + len(arrays)), out_specs=VME...]
where the time goes in v6:
time: 88.8 us; the launch traced here: 87.9 us
  waiting for transfers between devices  27.5 us (31%)
  blocking collectives  21.7 us (24%)
  Pallas kernels  19.9 us (22%)
  starting transfers between devices  17.9 us (20%)
    all_to_all x2, blocking collectives, exchange(): return lax.all_to_all(x, axes, split_axis=0, concat_axis=0, tiled=True)  21.7 us
    all_to_all x2, waiting for transfers between devices, exchange(): return lax.all_to_all(x, axes, split_axis=0, concat_axis=0, tiled=True)  17.1 us
    all_to_all x2, starting transfers between devices, exchange(): return lax.all_to_all(x, axes, split_axis=0, concat_axis=0, tiled=True)  11.7 us
    pallas_call x1, Pallas kernels, project(): pl.pallas_call(project_kernel, in_specs=[SMEM] * 2 + [HBM] * 3, out_specs...  11.3 us
    ppermute x3, waiting for transfers between devices, send_block(): return lax.ppermute(x, ('core', 'head'), pairs)  10.4 us
    pallas_call x2, Pallas kernels, attend(): pl.pallas_call(kernel, in_specs=[VMEM] * (1 + len(arrays)), out_specs=VME...  6.47 us
    ppermute x3, starting transfers between devices, send_block(): return lax.ppermute(x, ('core', 'head'), pairs)  5.22 us
  transfers between devices with their start and end apart: 10, of which 4 were waited for; matrix products, arithmetic and copies ran while one was open for 1% of the time, Pallas kernels for 9%

profile of v6, /device:TPU:0, one launch (start us, length us, event | category | flops | bytes accessed | tf_op | source)
XLA Modules:
  0.0 87.9 jit_solution(2715792602370311959)
XLA Ops:
  0.0 0.0 copy-start.1
  0.0 0.0 copy-start
  0.0 11.3 %project.1 = (bf16[2,512,128]{2,1,0:T(8,128)(2,1)S(1)}, bf16[2,512,128]{2,1,0:T(8,128)(2,1)S(1)}, bf16[2,512,128]{2,1,0:T(8,128)(2,1)S(1)}, bf16[2,512,128]{2,1,0:T(8,128)(2,1)S(1)}) custom-call(s32[1]{0:T(128)} %bitcast.1.head, s32[1]{0:T(128)S(6)} %sub.3.way, bf16[512,7680]{1,0:T(8,128)(2,1)} %x.1, bf16[7680,512]{1,0:T(8,128)(2,1)} %wk.1, bf16[7680,512]{1,0:T(8,128)(2,1)} %wv.1), custom_call_target="tpu_custom_call" | custom-call | tf_op jit(solution)/shard_map/project/pallas_call | solution.py:77
  11.4 2.9 %collective-permute-start.1 = (bf16[2,512,128]{2,1,0:T(8,128)(2,1)S(1)}, bf16[2,512,128]{2,1,0:T(8,128)(2,1)S(1)}, u32[]{:S(2)}, u32[]{:S(2)}) collective-permute-start(bf16[2,512,128]{2,1,0:T(8,128)(2,1)S(1)} %get-tuple-element.10), channel_id=1, source_target_pairs={{0,3},{1,0},{2,1},{3,2},{4,5},{5,6},{6,7},{7,4},{8,11},{9,8},{10,9... | collective-permute-start | bytes 786440 | tf_op jit(solution)/shard_map/ppermute | solution.py:267
  14.3 0.0 collective-permute-start.2
  14.3 2.3 %collective-permute-start.3 = (bf16[2,512,128]{2,1,0:T(8,128)(2,1)S(1)}, bf16[2,512,128]{2,1,0:T(8,128)(2,1)S(1)}, u32[]{:S(2)}, u32[]{:S(2)}) collective-permute-start(bf16[2,512,128]{2,1,0:T(8,128)(2,1)S(1)} %get-tuple-element.12), channel_id=1, source_target_pairs={{0,2},{1,3},{2,0},{3,1},{4,6},{5,7},{6,4},{7,5},{8,10},{9,11},{10,... | collective-permute-start | bytes 786440 | tf_op jit(solution)/shard_map/ppermute | solution.py:267
  16.6 0.0 collective-permute-start
  16.6 9.0 %collective-permute-done.1.rest_0_ = bf16[2,512,128]{2,1,0:T(8,128)(2,1)S(1)} collective-permute-done((bf16[2,512,128]{2,1,0:T(8,128)(2,1)S(1)}, bf16[2,512,128]{2,1,0:T(8,128)(2,1)S(1)}, u32[]{:S(2)}, u32[]{:S(2)}) %collective-permute-start.1) | collective-permute-done | bytes 262176 | tf_op jit(solution)/shard_map/ppermute | solution.py:267
  25.6 0.0 collective-permute-start.4
  25.6 0.0 collective-permute-done.2.rest_1_
  25.6 0.5 collective-permute-start.5
  26.1 1.4 %collective-permute-done.3.rest_2_ = bf16[2,512,128]{2,1,0:T(8,128)(2,1)S(1)} collective-permute-done((bf16[2,512,128]{2,1,0:T(8,128)(2,1)S(1)}, bf16[2,512,128]{2,1,0:T(8,128)(2,1)S(1)}, u32[]{:S(2)}, u32[]{:S(2)}) %collective-permute-start.3) | collective-permute-done | bytes 262176 | tf_op jit(solution)/shard_map/ppermute | solution.py:267
  27.5 0.0 collective-permute-start.6
  27.5 0.0 copy-done.1
  27.5 0.7 broadcast_in_dim.2
  28.2 8.0 %all-to-all-start = ((bf16[16,8,1024]{2,1,0:T(8,128)(2,1)}), bf16[16,8,1024]{2,1,0:T(8,128)(2,1)S(1)}, u32[]{:S(2)}, u32[]{:S(2)}) async-start(bf16[16,8,1024]{2,1,0:T(8,128)(2,1)} %broadcast_in_dim.2), calls=%async_computation | async-start | bytes 524288 | tf_op jit(solution)/shard_map/all_to_all | solution.py:258
  36.3 0.0 copy-done
  36.3 0.5 collective-permute-start.7
  36.8 8.7 %all-to-all-done.q = bf16[16,8,1024]{2,1,0:T(8,128)(2,1)S(1)} async-done(((bf16[16,8,1024]{2,1,0:T(8,128)(2,1)}), bf16[16,8,1024]{2,1,0:T(8,128)(2,1)S(1)}, u32[]{:S(2)}, u32[]{:S(2)}) %all-to-all-start) | async-done | bytes 262176 | tf_op jit(solution)/shard_map/all_to_all | solution.py:258
  45.5 0.0 collective-permute-done.rest_1_
  45.5 1.7 %attend.2.begun = f32[1024,256]{1,0:T(8,128)S(1)} custom-call(bf16[16,8,1024]{2,1,0:T(8,128)(2,1)S(1)} %all-to-all-done.q, bf16[2,512,128]{2,1,0:T(8,128)(2,1)S(1)} %get-tuple-element.9.rest_0_, bf16[2,512,128]{2,1,0:T(8,128)(2,1)S(1)} %collective-permute-done.rest_1_), custom_call_target="tpu_custom_call" | custom-call | tf_op jit(solution)/shard_map/attend/pallas_call | solution.py:169
  47.1 0.0 collective-permute-done.4.rest_3_
  47.1 0.0 collective-permute-done.5.rest_4_
  47.2 0.0 collective-permute-done.6.rest_5_
  47.2 4.8 %attend.3 = bf16[16,9,8,128]{3,2,1,0:T(8,128)(2,1)S(1)} custom-call(bf16[16,8,1024]{2,1,0:T(8,128)(2,1)S(1)} %all-to-all-done.q, f32[1024,256]{1,0:T(8,128)S(1)} %attend.2.begun, bf16[2,512,128]{2,1,0:T(8,128)(2,1)S(1)} %collective-permute-done.1.rest_0_, bf16[2,512,128]{2,1,0:T(8,128)(2,1)S(1)} %collective-permute-done.2.rest_1_, ...), custom_call_target="tpu_custom_call" | custom-call | tf_op jit(solution)/shard_map/attend/pallas_call | solution.py:169
  52.0 12.1 %all_to_all.20.parts = bf16[16,9,8,128]{3,2,1,0:T(8,128)(2,1)S(1)} all-to-all(bf16[16,9,8,128]{3,2,1,0:T(8,128)(2,1)S(1)} %attend.3), channel_id=1, replica_groups=mesh['y'=4,'z'=4,'core'=2,'head'=4] {'y','z'}, dimensions={0} | all-to-all | bytes 589824 | tf_op jit(solution)/shard_map/all_to_all | solution.py:258
  64.1 1.1 %combine.1 = bf16[16,8,1024]{2,1,0:T(8,128)(2,1)} custom-call(bf16[16,9,8,128]{3,2,1,0:T(8,128)(2,1)S(1)} %all_to_all.20.parts), custom_call_target="tpu_custom_call" | custom-call | tf_op jit(solution)/shard_map/combine/pallas_call | solution.py:201
  65.2 3.6 %all-to-all-start.2 = ((bf16[16,8,1024]{2,1,0:T(8,128)(2,1)}), bf16[16,8,1024]{2,1,0:T(8,128)(2,1)S(1)}, u32[]{:S(2)}, u32[]{:S(2)}) async-start(bf16[16,8,1024]{2,1,0:T(8,128)(2,1)} %combine.1), calls=%async_computation.2 | async-start | bytes 524288 | tf_op jit(solution)/shard_map/all_to_all | solution.py:258
  68.9 0.0 collective-permute-done.7.other
  68.9 8.5 %all-to-all-done.2.rows = bf16[16,8,1024]{2,1,0:T(8,128)(2,1)S(1)} async-done(((bf16[16,8,1024]{2,1,0:T(8,128)(2,1)}), bf16[16,8,1024]{2,1,0:T(8,128)(2,1)S(1)}, u32[]{:S(2)}, u32[]{:S(2)}) %all-to-all-start.2) | async-done | bytes 262176 | tf_op jit(solution)/shard_map/all_to_all | solution.py:258
  77.3 0.3 mix.1
  77.6 9.6 %all_to_all.21 = bf16[8,32,256]{2,1,0:T(8,128)(2,1)S(1)} all-to-all(bf16[8,32,256]{2,1,0:T(8,128)(2,1)S(1)} %bitcast.5), channel_id=1, replica_groups=mesh['y'=4,'z'=4,'core'=2,'head'=4] {'head','core'}, dimensions={0} | all-to-all | bytes 262144 | tf_op jit(solution)/shard_map/all_to_all | solution.py:258
  87.2 0.6 total.1
Async XLA Ops:
  0.0 27.5 %copy-start.1 = (bf16[8,1024]{1,0:T(8,128)(2,1)S(1)}, bf16[8,1024]{1,0:T(8,128)(2,1)}, u32[]{:S(2)}) copy-start(bf16[8,1024]{1,0:T(8,128)(2,1)} %param.8) | copy-start | bytes 49156
  0.0 36.3 %copy-start = (bf16[1024,256]{1,0:T(8,128)(2,1)S(1)}, bf16[1024,256]{1,0:T(8,128)(2,1)}, u32[]{:S(2)}) copy-start(bf16[1024,256]{1,0:T(8,128)(2,1)} %own.1) | copy-start | bytes 1572868
  11.4 14.2 %collective-permute-start.1 = (bf16[2,512,128]{2,1,0:T(8,128)(2,1)S(1)}, bf16[2,512,128]{2,1,0:T(8,128)(2,1)S(1)}, u32[]{:S(2)}, u32[]{:S(2)}) collective-permute-start(bf16[2,512,128]{2,1,0:T(8,128)(2,1)S(1)} %get-tuple-element.10), channel_id=1, source_target_pairs={{0,3},{1,0},{2,1},{3,2},{4,5},{5,6},{6,7},{7,4},{8,11},{9,8},{10,9... | collective-permute-start | bytes 786440 | tf_op jit(solution)/shard_map/ppermute | solution.py:267
  14.3 11.3 %collective-permute-start.2 = (bf16[2,512,128]{2,1,0:T(8,128)(2,1)S(1)}, bf16[2,512,128]{2,1,0:T(8,128)(2,1)S(1)}, u32[]{:S(2)}, u32[]{:S(2)}) collective-permute-start(bf16[2,512,128]{2,1,0:T(8,128)(2,1)S(1)} %get-tuple-element.11), channel_id=1, source_target_pairs={{0,1},{1,2},{2,3},{3,0},{4,7},{5,4},{6,5},{7,6},{8,9},{9,10},{10,1... | collective-permute-start | bytes 786440 | tf_op jit(solution)/shard_map/ppermute | solution.py:267
  14.3 13.2 %collective-permute-start.3 = (bf16[2,512,128]{2,1,0:T(8,128)(2,1)S(1)}, bf16[2,512,128]{2,1,0:T(8,128)(2,1)S(1)}, u32[]{:S(2)}, u32[]{:S(2)}) collective-permute-start(bf16[2,512,128]{2,1,0:T(8,128)(2,1)S(1)} %get-tuple-element.12), channel_id=1, source_target_pairs={{0,2},{1,3},{2,0},{3,1},{4,6},{5,7},{6,4},{7,5},{8,10},{9,11},{10,... | collective-permute-start | bytes 786440 | tf_op jit(solution)/shard_map/ppermute | solution.py:267
  16.6 28.9 %collective-permute-start = (bf16[2,512,128]{2,1,0:T(8,128)(2,1)S(1)}, bf16[2,512,128]{2,1,0:T(8,128)(2,1)S(1)}, u32[]{:S(2)}, u32[]{:S(2)}) collective-permute-start(bf16[2,512,128]{2,1,0:T(8,128)(2,1)S(1)} %get-tuple-element.9.rest_0_), channel_id=1, source_target_pairs={{0,4},{4,0},{1,5},{5,1},{2,6},{6,2},{3,7},{7,3},{8,12},{12,8},{9,1... | collective-permute-start | bytes 786440 | tf_op jit(solution)/shard_map/ppermute | solution.py:254
  25.6 21.6 %collective-permute-start.4 = (bf16[2,512,128]{2,1,0:T(8,128)(2,1)S(1)}, bf16[2,512,128]{2,1,0:T(8,128)(2,1)S(1)}, u32[]{:S(2)}, u32[]{:S(2)}) collective-permute-start(bf16[2,512,128]{2,1,0:T(8,128)(2,1)S(1)} %collective-permute-done.1.rest_0_), channel_id=1, source_target_pairs={{0,4},{4,0},{1,5},{5,1},{2,6},{6,2},{3,7},{7,3},{8,12},{12,8},{9,1... | collective-permute-start | bytes 786440 | tf_op jit(solution)/shard_map/ppermute | solution.py:254
  25.6 21.6 %collective-permute-start.5 = (bf16[2,512,128]{2,1,0:T(8,128)(2,1)S(1)}, bf16[2,512,128]{2,1,0:T(8,128)(2,1)S(1)}, u32[]{:S(2)}, u32[]{:S(2)}) collective-permute-start(bf16[2,512,128]{2,1,0:T(8,128)(2,1)S(1)} %collective-permute-done.2.rest_1_), channel_id=1, source_target_pairs={{0,4},{4,0},{1,5},{5,1},{2,6},{6,2},{3,7},{7,3},{8,12},{12,8},{9,1... | collective-permute-start | bytes 786440 | tf_op jit(solution)/shard_map/ppermute | solution.py:254
  27.5 19.7 %collective-permute-start.6 = (bf16[2,512,128]{2,1,0:T(8,128)(2,1)S(1)}, bf16[2,512,128]{2,1,0:T(8,128)(2,1)S(1)}, u32[]{:S(2)}, u32[]{:S(2)}) collective-permute-start(bf16[2,512,128]{2,1,0:T(8,128)(2,1)S(1)} %collective-permute-done.3.rest_2_), channel_id=1, source_target_pairs={{0,4},{4,0},{1,5},{5,1},{2,6},{6,2},{3,7},{7,3},{8,12},{12,8},{9,1... | collective-permute-start | bytes 786440 | tf_op jit(solution)/shard_map/ppermute | solution.py:254
  28.2 17.2 %all-to-all-start = ((bf16[16,8,1024]{2,1,0:T(8,128)(2,1)}), bf16[16,8,1024]{2,1,0:T(8,128)(2,1)S(1)}, u32[]{:S(2)}, u32[]{:S(2)}) async-start(bf16[16,8,1024]{2,1,0:T(8,128)(2,1)} %broadcast_in_dim.2), calls=%async_computation | async-start | bytes 524288 | tf_op jit(solution)/shard_map/all_to_all | solution.py:258
  36.3 32.6 %collective-permute-start.7 = (bf16[1024,256]{1,0:T(8,128)(2,1)S(1)}, bf16[1024,256]{1,0:T(8,128)(2,1)S(1)}, u32[]{:S(2)}, u32[]{:S(2)}) collective-permute-start(bf16[1024,256]{1,0:T(8,128)(2,1)S(1)} %copy-done), channel_id=1, source_target_pairs={{0,4},{4,0},{1,5},{5,1},{2,6},{6,2},{3,7},{7,3},{8,12},{12,8},{9,1... | collective-permute-start | bytes 1572872 | tf_op jit(solution)/shard_map/ppermute | solution.py:254
  65.2 12.1 %all-to-all-start.2 = ((bf16[16,8,1024]{2,1,0:T(8,128)(2,1)}), bf16[16,8,1024]{2,1,0:T(8,128)(2,1)S(1)}, u32[]{:S(2)}, u32[]{:S(2)}) async-start(bf16[16,8,1024]{2,1,0:T(8,128)(2,1)} %combine.1), calls=%async_computation.2 | async-start | bytes 524288 | tf_op jit(solution)/shard_map/all_to_all | solution.py:258
